TPU v7x, 256 devices: a whole 4x4x8 slice. The times are simulated.
256 devices in a mesh: member: 4 (over y_hi, core), node: 64 (over y_lo, x, z).
Axes of the slice: x: 4, y: 4 (y_hi: 2, y_lo: 2; y = y_hi * 2 + y_lo), z: 8, core: 2. Of those that a mesh axis runs over, the one named last changes fastest.
Arguments:
- gridpoint_state: bfloat16 [218, 65536], P(None, 'node'), may hold values from -6 to 6
- grid_truth: bfloat16 [100, 65536], P(None, 'node'), may hold values from -6 to 6
- encoder_slots: int32 [16384, 16], P('node'), may hold values from 0 to 65535, as said below
- encoder_count: int32 [16384], P('node'), may hold values from 1 to 16
- node_reach: int32 [16384], P('node'), may hold values from 128 to 256
- decoder_slots: int32 [65536, 4], P('node'), may hold values from 0 to 16383, as said below
- member_perturb: bfloat16 [4, 16384, 1024], P('member', 'node'), may hold values from -6 to 6
- embed_weight: bfloat16 [218, 1024], replicated, may hold values from -0.4375 to 0.4375
- norm_gains: float32 [3, 1024], replicated, may hold values from 0.1 to 1.9
- qkv_weight: bfloat16 [1024, 3072], replicated
- out_weight: bfloat16 [1024, 1024], replicated, may hold values from -0.1875 to 0.1875
- up_weight: bfloat16 [1024, 4096], P('node'), may hold values from -0.1875 to 0.1875
- down_weight: bfloat16 [1024, 4096], P('node'), may hold values from -0.09375 to 0.09375
- head_weight: bfloat16 [1024, 100], replicated, may hold values from -0.1875 to 0.1875
Outputs:
- crps_grad: float32 [4, 100, 65536], P('member', None, 'node')
Inputs may be any that keep to these rules, and one draw needn't show every extreme that they name: `encoder_slots`: for a hidden node of region r (nodes r * 256 to (r + 1) * 256 - 1), every slot names a grid point of region r - 1, r or r + 1, a region holding 1024 consecutive points; slots from encoder_count on are padding. `decoder_slots`: for a grid point of region r, every slot names a hidden node of region r - 1, r or r + 1.
All inputs are finite; a program needn't handle non-finite values.
Results may differ from a plain program's by a relative error of at most 0.0095.
The roundings to bfloat16 on the way count: a program that leaves them out, or rounds other values in their place, can miss the bound.
Values may be sent and summed in bfloat16 or wider, within the bound.
No kernel may reach another device: no remote copies, remote signals or barrier semaphores. Data moves between devices by JAX's collectives and lax.ppermute only.
A program may use at most 128 MiB of HBM per device.

v0:
```python
import jax
import jax.numpy as jnp
from jax import lax
from jax.experimental import pallas as pl
from jax.experimental.pallas import tpu as pltpu
from jax.sharding import Mesh
from jax.sharding import PartitionSpec as P

HEADS = 16
HEAD_DIM = 64
BAND = 256
NODE = ("node_0", "node_1", "node_2")
MEMBER = ("member_hi", "member_core")

EPS = 1e-05
SMOOTH = 0.25

F32 = jnp.float32
BF16 = jnp.bfloat16
LANES_BOTH = (((1,), (1,)), ((), ()))


def params(mib):
    return pltpu.CompilerParams(vmem_limit_bytes=mib * 1024 * 1024)


SHORT = pl.CostEstimate(flops=1, bytes_accessed=1, transcendentals=0)


def layer_norm(entries, scale_gain):
    average = jnp.mean(entries, axis=-1, keepdims=True)
    centred = entries - average
    variance = jnp.mean(centred * centred, axis=-1, keepdims=True)
    return centred * lax.rsqrt(variance + EPS) * scale_gain


def score_gradient(difference):
    return difference * lax.rsqrt(difference * difference + SMOOTH * SMOOTH)


def dot(left_side, right_side):
    return jnp.dot(left_side, right_side, preferred_element_type=F32)


def dot_lanes(left_side, right_side):
    return lax.dot_general(left_side, right_side, LANES_BOTH, preferred_element_type=F32)


def neighbours(block):
    count = lax.axis_size(NODE)
    forward = [(i, (i + 1) % count) for i in range(count)]
    backward = [(target, source) for source, target in forward]
    return lax.ppermute(block, NODE, forward), lax.ppermute(block, NODE, backward)


def other_core(block):
    return lax.ppermute(block, "member_core", [(0, 1), (1, 0)])


def tally_kernel(place_ref, slots_ref, count_ref, out_ref):
    nodes = out_ref.shape[1]
    tall, rows = 256, 64
    slots = slots_ref[...] - place_ref[2]
    used = lax.broadcasted_iota(jnp.int32, slots.shape, 0) < count_ref[...]
    slots = jnp.where(used, slots, -1)
    high = slots >> 8
    low = (slots & 255).astype(F32)
    window = lax.broadcasted_iota(jnp.int32, (tall, nodes), 0).astype(F32).astype(BF16)
    one, zero = jnp.ones((), BF16), jnp.zeros((), BF16)

    def body(step, carry):
        first = pl.multiple_of(step * tall, tall)
        keys = jnp.where(high == step, low, -1.0).astype(BF16)
        for start in range(0, tall, rows):
            total = jnp.zeros((rows, nodes), BF16)
            for position in range(slots.shape[0]):
                hit = keys[position : position + 1, :] == window[start : start + rows, :]
                total = total + jnp.where(hit, one, zero)
            out_ref[pl.ds(first + start, rows), :] = total
        return carry

    lax.fori_loop(0, out_ref.shape[0] // tall, body, 0)


def encoder_tallies(place, slots, counts, width):
    count, nodes = slots.shape
    vmem = pl.BlockSpec(memory_space=pltpu.VMEM)
    return pl.pallas_call(
        tally_kernel,
        out_shape=jax.ShapeDtypeStruct((width, nodes), BF16),
        in_specs=[pl.BlockSpec(memory_space=pltpu.SMEM), vmem, vmem],
        compiler_params=params(16),
        cost_estimate=SHORT,
        name="encoder_tallies",
    )(place, slots, counts)


def pooled_kernel(tally_ref, low_ref, own_ref, high_ref, count_ref, out_ref):
    width = low_ref.shape[1]
    total = dot(own_ref[...], tally_ref[width : 2 * width, :])
    total = total + dot(low_ref[...], tally_ref[:width, :])
    total = total + dot(high_ref[...], tally_ref[2 * width :, :])
    out_ref[...] = (total / count_ref[...].astype(F32)).astype(BF16)


def pool(tallies, low, own, high, counts):
    nodes = tallies.shape[1]
    channels = own.shape[0]
    return pl.pallas_call(
        pooled_kernel,
        out_shape=jax.ShapeDtypeStruct((channels, nodes), BF16),
        compiler_params=params(24),
        cost_estimate=SHORT,
        name="pooled",
    )(tallies, low, own, high, counts)


def embed_kernel(pooled_ref, perturb_ref, embed_ref, gain_ref, start_ref, normed_ref):
    embedded = lax.dot_general(
        pooled_ref[...], embed_ref[...], (((0,), (0,)), ((), ())), preferred_element_type=F32
    )
    start = embedded + perturb_ref[...].astype(F32)
    start_ref[...] = start
    normed_ref[...] = layer_norm(start, gain_ref[0:1, :]).astype(BF16)


def embed(pooled, perturb, embed_weight, norm_gains):
    return pl.pallas_call(
        embed_kernel,
        out_shape=(
            jax.ShapeDtypeStruct(perturb.shape, F32),
            jax.ShapeDtypeStruct(perturb.shape, BF16),
        ),
        compiler_params=params(16),
        cost_estimate=SHORT,
        name="embed",
    )(pooled, perturb, embed_weight, norm_gains)


def qkv_kernel(low_ref, own_ref, high_ref, qkv_hbm, query_ref, kv_ref, qkv_ref, sem):
    copy = pltpu.make_async_copy(qkv_hbm, qkv_ref, sem)
    copy.start()
    nodes, width = own_ref.shape
    copy.wait()
    query = dot(own_ref[...], qkv_ref[:, :width]).astype(BF16)
    query_ref[...] = query * jnp.asarray(HEAD_DIM ** (-0.5), BF16)
    for place, normed in enumerate((low_ref, own_ref, high_ref)):
        for half in range(2):
            columns = slice((half + 1) * width, (half + 2) * width)
            kv_ref[place * nodes : (place + 1) * nodes, half * width : (half + 1) * width] = dot(
                normed[...], qkv_ref[:, columns]
            ).astype(BF16)


def qkv(low, own, high, qkv_weight):
    nodes, width = own.shape
    vmem = pl.BlockSpec(memory_space=pltpu.VMEM)
    return pl.pallas_call(
        qkv_kernel,
        out_shape=(
            jax.ShapeDtypeStruct((nodes, width), BF16),
            jax.ShapeDtypeStruct((3 * nodes, 2 * width), BF16),
        ),
        in_specs=[vmem] * 3 + [pl.BlockSpec(memory_space=pl.ANY)],
        scratch_shapes=[pltpu.VMEM(qkv_weight.shape, BF16), pltpu.SemaphoreType.DMA],
        compiler_params=params(32),
        cost_estimate=SHORT,
        name="qkv",
    )(low, own, high, qkv_weight)


def attention_kernel(
    where_ref, query_ref, kv_ref, reach_ref, start_ref, gain_ref, out_hbm,
    mid_ref, normed_ref, cap_ref, attended_ref, out_ref, sem,
):
    copy = pltpu.make_async_copy(out_hbm, out_ref, sem)
    copy.start()
    nodes, width = query_ref.shape
    rows = cap_ref.shape[1]
    span = cap_ref.shape[2]
    first_query = where_ref[0]
    node_total = where_ref[1]
    reaches = jnp.transpose(jnp.broadcast_to(reach_ref[...].astype(F32), (128, nodes)))
    for block in range(nodes // rows):
        at = first_query + block * rows + lax.broadcasted_iota(jnp.int32, (rows, span), 0)
        key = first_query - BAND + block * rows + lax.broadcasted_iota(jnp.int32, (rows, span), 1)
        reach = reaches[block * rows : (block + 1) * rows, :1].astype(jnp.int32)
        allowed = (jnp.abs(at - key) <= reach) & (key >= 0) & (key < node_total)
        cap_ref[block] = jnp.where(allowed, 3e38, -1e30)

    lane = lax.broadcasted_iota(jnp.int32, (1, 2 * HEAD_DIM), 1)
    for block in range(nodes // rows):
        cap = cap_ref.at[block]
        for pair in range(HEADS // 2):
            columns = slice(pair * 2 * HEAD_DIM, (pair + 1) * 2 * HEAD_DIM)
            value_columns = slice(width + pair * 2 * HEAD_DIM, width + (pair + 1) * 2 * HEAD_DIM)
            queries = query_ref[block * rows : (block + 1) * rows, columns]
            keys = kv_ref[block * rows : block * rows + span, columns]
            values = kv_ref[block * rows : block * rows + span, value_columns]
            halves = []
            for side in range(2):
                mine = (lane < HEAD_DIM) if side == 0 else (lane >= HEAD_DIM)
                chosen = jnp.where(mine, queries, jnp.zeros_like(queries))
                scores = jnp.minimum(dot_lanes(chosen, keys), cap[...])
                highest = jnp.max(scores, axis=-1, keepdims=True)
                weights = jnp.exp(scores - highest)
                total = jnp.sum(weights, axis=-1, keepdims=True)
                blended = dot(weights.astype(BF16), values)
                halves.append(blended * (1.0 / total))
            attended_ref[block * rows : (block + 1) * rows, columns] = jnp.where(
                lane < HEAD_DIM, halves[0], halves[1]
            ).astype(BF16)
    copy.wait()
    middle = start_ref[...] + dot(attended_ref[...], out_ref[...])
    mid_ref[...] = middle
    normed_ref[...] = layer_norm(middle, gain_ref[1:2, :]).astype(BF16)


def attention(where, query, kv, reach, start, norm_gains, out_weight):
    nodes, width = query.shape
    rows = 128
    span = rows + 2 * BAND
    vmem = pl.BlockSpec(memory_space=pltpu.VMEM)
    return pl.pallas_call(
        attention_kernel,
        out_shape=(
            jax.ShapeDtypeStruct((nodes, width), F32),
            jax.ShapeDtypeStruct((nodes, width), BF16),
        ),
        in_specs=[pl.BlockSpec(memory_space=pltpu.SMEM)]
        + [vmem] * 5
        + [pl.BlockSpec(memory_space=pl.ANY)],
        scratch_shapes=[
            pltpu.VMEM((nodes // rows, rows, span), F32),
            pltpu.VMEM((nodes, width), BF16),
            pltpu.VMEM(out_weight.shape, BF16),
            pltpu.SemaphoreType.DMA,
        ],
        compiler_params=params(32),
        cost_estimate=SHORT,
        name="attention",
    )(where, query, kv, reach, start, norm_gains, out_weight)


def in_order_kernel(place_ref, *refs):
    count = len(refs) - 2
    for shift in range(count):
        at = lax.rem(place_ref[4] + shift, count)
        for side in range(2):
            refs[count + side][at] = refs[shift][side]


def in_order(place, blocks):
    count = len(blocks)
    vmem = pl.BlockSpec(memory_space=pltpu.VMEM)
    return pl.pallas_call(
        in_order_kernel,
        out_shape=(jax.ShapeDtypeStruct((count,) + blocks[0].shape[1:], BF16),) * 2,
        in_specs=[pl.BlockSpec(memory_space=pltpu.SMEM)] + [vmem] * count,
        compiler_params=params(24),
        cost_estimate=SHORT,
        name="shards_in_order",
    )(place, *blocks)


def mlp_kernel(place_ref, own_ref, other_ref, *refs):
    blocks = refs[:8]
    own_out, other_out, tokens_ref, total_ref = refs[8:]
    nodes, width = own_ref.shape
    part = width // 8
    hidden = blocks[0].shape[2]
    rows = blocks[0].shape[1] // 2
    step = 512

    def at(block):
        along_x = lax.rem(place_ref[3] + (0, 3, 1, 2)[block % 4], 4)
        along_y = place_ref[5] if block < 4 else 1 - place_ref[5]
        return pl.ds(pl.multiple_of((along_y * 4 + along_x) * part, part), part)

    for block in range(8):
        columns = slice(block * part, (block + 1) * part)
        tokens_ref[:nodes, columns] = other_ref[:, at(block)]
        tokens_ref[nodes:, columns] = own_ref[:, at(block)]

    def all_rows(first, chosen):
        pieces = []
        for block in blocks:
            piece = block[:, first : first + rows, chosen]
            pieces.append(piece.reshape(piece.shape[0] * rows, step))
        return jnp.concatenate(pieces, axis=0)

    for start in range(0, hidden, step):
        chosen = slice(start, start + step)
        upper = dot(tokens_ref[...], all_rows(0, chosen))
        active = jax.nn.gelu(upper).astype(BF16)
        lowered = dot_lanes(active, all_rows(rows, chosen))
        if start == 0:
            total_ref[...] = lowered
        else:
            total_ref[...] += lowered
    for block in range(8):
        columns = slice(block * part, (block + 1) * part)
        other_out[:, at(block)] = total_ref[:nodes, columns]
        own_out[:, at(block)] = total_ref[nodes:, columns]


def mlp_parts(place, own, other, blocks):
    nodes, width = own.shape
    hidden = blocks[0].shape[2]
    vmem = pl.BlockSpec(memory_space=pltpu.VMEM)
    return pl.pallas_call(
        mlp_kernel,
        out_shape=(jax.ShapeDtypeStruct((nodes, width), F32),) * 2,
        in_specs=[pl.BlockSpec(memory_space=pltpu.SMEM)] + [vmem] * (2 + len(blocks)),
        scratch_shapes=[
            pltpu.VMEM((2 * nodes, width), BF16),
            pltpu.VMEM((2 * nodes, width), F32),
        ],
        compiler_params=params(40),
        cost_estimate=SHORT,
        name="mlp_parts",
    )(place, own, other, *blocks)


def turn(block, axis, step):
    count = lax.axis_size(axis)
    return lax.ppermute(block, axis, [(i, (i + step) % count) for i in range(count)])


def beside(block):
    return lax.ppermute(block, NODE[0], [(0, 1), (1, 0)])


def across(block):
    return lax.ppermute(block, (MEMBER[0], NODE[0]), [(0, 3), (3, 0), (1, 2), (2, 1)])


def head_kernel(mid_ref, own_ref, other_ref, gain_ref, head_ref, out_ref):
    ending = mid_ref[...] + (own_ref[...] + other_ref[...])
    final = layer_norm(ending, gain_ref[2:3, :]).astype(BF16)
    out_ref[...] = dot_lanes(head_ref[...], final).astype(BF16)


def head(middle, own, other, norm_gains, head_rows):
    nodes, width = middle.shape
    variables = head_rows.shape[0]
    return pl.pallas_call(
        head_kernel,
        out_shape=jax.ShapeDtypeStruct((variables, nodes), BF16),
        compiler_params=params(24),
        cost_estimate=SHORT,
        name="final_head",
    )(middle, own, other, norm_gains, head_rows)


def decoder_tally_kernel(place_ref, slots_ref, out_ref):
    rows = 64
    points = out_ref.shape[1]
    slots = slots_ref.shape[0]

    def body(step, carry):
        first = pl.multiple_of(step * rows, rows)
        node = first + place_ref[7] + lax.broadcasted_iota(jnp.int32, (rows, points), 0)
        total = jnp.zeros((rows, points), F32)
        for position in range(slots):
            hit = slots_ref[position : position + 1, :] == node
            total = total + jnp.where(hit, 1.0 / slots, 0.0)
        out_ref[pl.ds(first, rows), :] = total.astype(BF16)
        return carry

    lax.fori_loop(0, out_ref.shape[0] // rows, body, 0)


def decoder_tallies(place, slots, nodes):
    count, points = slots.shape
    return pl.pallas_call(
        decoder_tally_kernel,
        in_specs=[
            pl.BlockSpec(memory_space=pltpu.SMEM),
            pl.BlockSpec(memory_space=pltpu.VMEM),
        ],
        out_shape=jax.ShapeDtypeStruct((nodes, points), BF16),
        compiler_params=params(16),
        cost_estimate=SHORT,
        name="decoder_tallies",
    )(place, slots)


def crps_kernel(tally_ref, state_ref, truth_ref, *refs):
    out_ref, forecast_ref = refs[-2:]
    field_refs = refs[:-2]
    per_ref, padded, nodes = field_refs[0].shape
    variables = truth_ref.shape[0]
    state = state_ref[:variables, :].astype(F32)
    members = 0
    for first in range(0, len(field_refs), 3):
        delta = None
        for at in range(3):
            stacked = field_refs[first + at][...].reshape(per_ref * padded, nodes)
            term = dot(stacked, tally_ref[at * nodes : (at + 1) * nodes, :])
            delta = term if delta is None else delta + term
        for k in range(per_ref):
            forecast_ref[members] = state + delta[k * padded : k * padded + variables]
            members += 1
    own = forecast_ref[0]
    pairwise = None
    for member in range(members):
        term = score_gradient(own - forecast_ref[member])
        pairwise = term if pairwise is None else pairwise + term
    gradient = score_gradient(own - truth_ref[...].astype(F32)) * (1.0 / members) - pairwise * (
        1.0 / (members * (members - 1))
    )
    out_ref[...] = gradient[:, None, :]


def crps(tallies, state, truth, fields):
    variables, points = truth.shape
    members = len(fields) // 3 * fields[0].shape[0]
    return pl.pallas_call(
        crps_kernel,
        out_shape=jax.ShapeDtypeStruct((variables, 1, points), F32),
        scratch_shapes=[pltpu.VMEM((members, variables, points), F32)],
        compiler_params=params(32),
        cost_estimate=SHORT,
        name="decoder_crps",
    )(tallies, state, truth, *fields)


def per_device(
    gridpoint_state,
    grid_truth,
    encoder_slots,
    encoder_count,
    node_reach,
    decoder_slots,
    member_perturb,
    embed_weight,
    norm_gains,
    qkv_weight,
    out_weight,
    up_weight,
    down_weight,
    head_weight,
):
    region = lax.axis_index(NODE)
    region_count = lax.axis_size(NODE)
    core = lax.axis_index("member_core")
    grid_dev = gridpoint_state.shape[1]
    node_dev = encoder_slots.shape[0]
    hidden = up_weight.shape[1] // 2
    perturb = member_perturb[0]

    place = jnp.stack(
        [
            region * node_dev,
            region_count * node_dev,
            (region - 1) * grid_dev,
            lax.axis_index(NODE[1]),
            lax.axis_index(NODE[2]),
            lax.axis_index(NODE[0]),
            lax.axis_index(MEMBER),
            (region - 1) * node_dev,
        ]
    ).astype(jnp.int32)

    share = jnp.concatenate(
        [
            lax.dynamic_slice_in_dim(up_weight, core * hidden, hidden, 1),
            lax.dynamic_slice_in_dim(down_weight, core * hidden, hidden, 1),
        ],
        axis=0,
    )
    counts = encoder_count[None, :]
    tie = lax.optimization_barrier

    far_share = turn(share, NODE[1], 2)
    state_low, state_high = neighbours(gridpoint_state)
    tallies = encoder_tallies(place, encoder_slots.T, counts, 3 * grid_dev)
    tallies, far_share = tie((tallies, far_share))
    both = jnp.stack([share, far_share])
    ahead, behind = [turn(both, NODE[2], 1)], [turn(both, NODE[2], -1)]
    pooled = pool(tallies, state_low, gridpoint_state, state_high, counts)
    pooled, ahead[0], behind[0] = tie((pooled, ahead[0], behind[0]))
    start, normed = embed(pooled, perturb, embed_weight, norm_gains)
    for _ in range(2):
        ahead.append(turn(ahead[-1], NODE[2], 1))
        behind.append(turn(behind[-1], NODE[2], -1))
    start, normed, ahead[2], behind[2] = tie((start, normed, ahead[2], behind[2]))
    normed_low, normed_high = neighbours(normed)
    ahead.append(turn(ahead[-1], NODE[2], 1))
    column, far = in_order(place, [both] + behind + ahead[::-1])

    before = turn(column, NODE[1], 1)
    after = turn(column, NODE[1], -1)
    other_column = beside(column)
    other_far = across(far)
    normed_low, normed_high, before, after, other_column, other_far = tie(
        (normed_low, normed_high, before, after, other_column, other_far)
    )

    other_before = beside(before)
    other_after = across(after)
    query, kv = qkv(normed_low, normed, normed_high, qkv_weight)
    decoder_near = decoder_tallies(place, decoder_slots.T, 3 * node_dev)
    middle, normed_mid = attention(
        place, query, kv, node_reach[None, :], start, norm_gains, out_weight
    )
    shards = (
        column,
        before,
        after,
        far,
        other_column,
        other_before,
        other_after,
        other_far,
    )

    normed_other = other_core(normed_mid)
    part_mine, part_other = mlp_parts(place, normed_mid, normed_other, shards)
    head_rows = jnp.pad(head_weight.T, ((0, -head_weight.shape[1] % 16), (0, 0)))
    projected = head(middle, part_mine, other_core(part_other), norm_gains, head_rows)

    chip = jnp.stack([projected, other_core(projected)])
    fields = jnp.concatenate([chip, lax.ppermute(chip, MEMBER[0], [(0, 1), (1, 0)])])
    fields_low, fields_high = neighbours(fields)
    gradient = crps(
        decoder_near, gridpoint_state, grid_truth, (fields_low, fields, fields_high)
    )
    return gradient.transpose(1, 0, 2)


def solution(mesh):
    torus = Mesh(
        mesh.devices.reshape(2, 2, 2, 4, 8),
        MEMBER + NODE,
    )
    return jax.shard_map(
        per_device,
        mesh=torus,
        in_specs=(
            P(None, NODE),
            P(None, NODE),
            P(NODE, None),
            P(NODE),
            P(NODE),
            P(NODE, None),
            P(MEMBER, NODE, None),
            P(),
            P(),
            P(),
            P(),
            P(NODE, None),
            P(NODE, None),
            P(),
        ),
        out_specs=P(MEMBER, None, NODE),
        check_vma=False,
    )
```

profile of v0, /device:TPU:8, one launch (start us, length us, event | category | flops | bytes accessed | tf_op | source)
XLA Modules:
  0.0 141.4 jit_solution(4421293569447730646)
XLA Ops:
  0.0 0.9 constant_dynamic-slice_fusion
  1.0 3.1 %collective-permute-start = (bf16[32,2048]{1,0:T(8,128)(2,1)S(1)}, bf16[32,2048]{1,0:T(8,128)(2,1)S(1)}, u32[]{:S(2)}, u32[]{:S(2)}) collective-permute-start(bf16[32,2048]{1,0:T(8,128)(2,1)S(1)} %get-tuple-element.56), channel_id=1, source_target_pairs={{0,16},{8,24},{16,0},{24,8},{1,17},{9,25},{17,1},{25,9},{2,18},{10... | collective-permute-start | bytes 393224 | tf_op jit(solution)/shard_map/ppermute | solution.py:327
  4.1 1.9 %collective-permute-start.1 = (bf16[218,1024]{1,0:T(8,128)(2,1)}, bf16[218,1024]{1,0:T(8,128)(2,1)S(1)}, u32[]{:S(2)}, u32[]{:S(2)}) collective-permute-start(bf16[218,1024]{1,0:T(8,128)(2,1)} %state_ref.1), channel_id=1, source_target_pairs={{0,1},{1,2},{2,3},{3,4},{4,5},{5,6},{6,7},{7,8},{8,9},{9,10},{10,1... | collective-permute-start | bytes 1339400 | tf_op jit(solution)/shard_map/ppermute | solution.py:53
  6.0 4.4 %collective-permute-start.2 = (bf16[218,1024]{1,0:T(8,128)(2,1)}, bf16[218,1024]{1,0:T(8,128)(2,1)S(1)}, u32[]{:S(2)}, u32[]{:S(2)}) collective-permute-start(bf16[218,1024]{1,0:T(8,128)(2,1)} %state_ref.1), channel_id=1, source_target_pairs={{1,0},{2,1},{3,2},{4,3},{5,4},{6,5},{7,6},{8,7},{9,8},{10,9},{11,1... | collective-permute-start | bytes 1339400 | tf_op jit(solution)/shard_map/ppermute | solution.py:53
  10.4 0.1 stack.49.place_ref.where_ref
  10.5 0.7 copy-done.7
  11.2 0.7 copy-done.9
  11.9 3.2 %encoder_tallies.1.tally_ref = bf16[3072,256]{1,0:T(8,128)(2,1)S(1)} custom-call(s32[8]{0:T(128)S(1)} %stack.49.place_ref.where_ref, s32[16,256]{1,0:T(8,128)S(1)} %bitcast.22, s32[1,256]{1,0:T(1,128)S(1)} %bitcast.24), custom_call_target="tpu_custom_call" | custom-call | flops 1 | bytes 1 | tf_op jit(solution)/shard_map/encoder_tallies/pallas_call | solution.py:88
  15.1 0.0 copy-start.4
  15.1 0.0 copy-start.6
  15.1 0.0 collective-permute-done
  15.1 0.0 copy-start
  15.2 0.1 collective-permute-start.3
  15.3 3.2 %collective-permute-start.4 = (bf16[2,32,2048]{2,1,0:T(8,128)(2,1)S(1)}, bf16[2,32,2048]{2,1,0:T(8,128)(2,1)S(1)}, u32[]{:S(2)}, u32[]{:S(2)}) collective-permute-start(bf16[2,32,2048]{2,1,0:T(8,128)(2,1)S(1)} %pad_maximum_fusion.refs_0_), channel_id=1, source_target_pairs={{0,7},{1,0},{2,1},{3,2},{4,3},{5,4},{6,5},{7,6},{8,15},{9,8},{10,9... | collective-permute-start | bytes 786440 | tf_op jit(solution)/shard_map/ppermute | solution.py:327
  18.5 3.5 %collective-permute-done.1.low_ref = bf16[218,1024]{1,0:T(8,128)(2,1)S(1)} collective-permute-done((bf16[218,1024]{1,0:T(8,128)(2,1)}, bf16[218,1024]{1,0:T(8,128)(2,1)S(1)}, u32[]{:S(2)}, u32[]{:S(2)}) %collective-permute-start.1) | collective-permute-done | bytes 446496 | tf_op jit(solution)/shard_map/ppermute | solution.py:53
  22.0 0.0 collective-permute-done.2.high_ref
  22.0 0.5 pooled.1.pooled_ref
  22.5 3.5 %collective-permute-done.3.refs_7_ = bf16[2,32,2048]{2,1,0:T(8,128)(2,1)S(1)} collective-permute-done((bf16[2,32,2048]{2,1,0:T(8,128)(2,1)S(1)}, bf16[2,32,2048]{2,1,0:T(8,128)(2,1)S(1)}, u32[]{:S(2)}, u32[]{:S(2)}) %collective-permute-start.3) | collective-permute-done | bytes 262176 | tf_op jit(solution)/shard_map/ppermute | solution.py:327
  26.0 0.0 collective-permute-done.4.refs_1_
  26.0 0.0 collective-permute-start.5
  26.0 3.4 %collective-permute-start.7 = (bf16[2,32,2048]{2,1,0:T(8,128)(2,1)S(1)}, bf16[2,32,2048]{2,1,0:T(8,128)(2,1)S(1)}, u32[]{:S(2)}, u32[]{:S(2)}) collective-permute-start(bf16[2,32,2048]{2,1,0:T(8,128)(2,1)S(1)} %collective-permute-done.4.refs_1_), channel_id=1, source_target_pairs={{0,7},{1,0},{2,1},{3,2},{4,3},{5,4},{6,5},{7,6},{8,15},{9,8},{10,9... | collective-permute-start | bytes 786440 | tf_op jit(solution)/shard_map/ppermute | solution.py:327
  29.4 5.1 %collective-permute-done.5.refs_6_ = bf16[2,32,2048]{2,1,0:T(8,128)(2,1)S(1)} collective-permute-done((bf16[2,32,2048]{2,1,0:T(8,128)(2,1)S(1)}, bf16[2,32,2048]{2,1,0:T(8,128)(2,1)S(1)}, u32[]{:S(2)}, u32[]{:S(2)}) %collective-permute-start.5) | collective-permute-done | bytes 262176 | tf_op jit(solution)/shard_map/ppermute | solution.py:327
  34.5 0.0 collective-permute-start.6
  34.5 0.0 collective-permute-done.7.refs_2_
  34.5 3.2 %collective-permute-start.8 = (bf16[2,32,2048]{2,1,0:T(8,128)(2,1)S(1)}, bf16[2,32,2048]{2,1,0:T(8,128)(2,1)S(1)}, u32[]{:S(2)}, u32[]{:S(2)}) collective-permute-start(bf16[2,32,2048]{2,1,0:T(8,128)(2,1)S(1)} %collective-permute-done.7.refs_2_), channel_id=1, source_target_pairs={{0,7},{1,0},{2,1},{3,2},{4,3},{5,4},{6,5},{7,6},{8,15},{9,8},{10,9... | collective-permute-start | bytes 786440 | tf_op jit(solution)/shard_map/ppermute | solution.py:327
  37.8 0.6 embed.1
  38.4 3.7 %collective-permute-done.6.refs_5_ = bf16[2,32,2048]{2,1,0:T(8,128)(2,1)S(1)} collective-permute-done((bf16[2,32,2048]{2,1,0:T(8,128)(2,1)S(1)}, bf16[2,32,2048]{2,1,0:T(8,128)(2,1)S(1)}, u32[]{:S(2)}, u32[]{:S(2)}) %collective-permute-start.6) | collective-permute-done | bytes 262176 | tf_op jit(solution)/shard_map/ppermute | solution.py:327
  42.1 0.5 collective-permute-done.8.refs_3_
  42.6 0.0 collective-permute-start.11
  42.6 5.4 %collective-permute-start.10 = (bf16[256,1024]{1,0:T(8,128)(2,1)S(1)}, bf16[256,1024]{1,0:T(8,128)(2,1)S(1)}, u32[]{:S(2)}, u32[]{:S(2)}) collective-permute-start(bf16[256,1024]{1,0:T(8,128)(2,1)S(1)} %get-tuple-element.37.own_ref), channel_id=1, source_target_pairs={{1,0},{2,1},{3,2},{4,3},{5,4},{6,5},{7,6},{8,7},{9,8},{10,9},{11,1... | collective-permute-start | bytes 1572872 | tf_op jit(solution)/shard_map/ppermute | solution.py:53
  48.0 2.6 %collective-permute-done.11.refs_4_ = bf16[2,32,2048]{2,1,0:T(8,128)(2,1)S(1)} collective-permute-done((bf16[2,32,2048]{2,1,0:T(8,128)(2,1)S(1)}, bf16[2,32,2048]{2,1,0:T(8,128)(2,1)S(1)}, u32[]{:S(2)}, u32[]{:S(2)}) %collective-permute-start.11) | collective-permute-done | bytes 262176 | tf_op jit(solution)/shard_map/ppermute | solution.py:327
  50.6 0.7 shards_in_order.1
  51.3 7.5 %collective-permute-start.12 = (bf16[8,32,2048]{2,1,0:T(8,128)(2,1)S(1)}, bf16[8,32,2048]{2,1,0:T(8,128)(2,1)S(1)}, u32[]{:S(2)}, u32[]{:S(2)}) collective-permute-start(bf16[8,32,2048]{2,1,0:T(8,128)(2,1)S(1)} %get-tuple-element.40.refs_0_), channel_id=1, source_target_pairs={{0,8},{8,16},{16,24},{24,0},{1,9},{9,17},{17,25},{25,1},{2,10},{10... | collective-permute-start | bytes 3145736 | tf_op jit(solution)/shard_map/ppermute | solution.py:327
  58.8 0.0 collective-permute-start.13
  58.8 0.2 collective-permute-start.14
  59.0 3.6 %collective-permute-start.15 = (bf16[8,32,2048]{2,1,0:T(8,128)(2,1)S(1)}, bf16[8,32,2048]{2,1,0:T(8,128)(2,1)S(1)}, u32[]{:S(2)}, u32[]{:S(2)}) collective-permute-start(bf16[8,32,2048]{2,1,0:T(8,128)(2,1)S(1)} %get-tuple-element.41.refs_3_), channel_id=1, source_target_pairs={{0,160},{160,0},{32,128},{128,32},{1,161},{161,1},{33,129},{129,33... | collective-permute-start | bytes 3145736 | tf_op jit(solution)/shard_map/ppermute | solution.py:335
  62.6 0.0 collective-permute-done.10.high_ref
  62.6 0.0 collective-permute-start.9
  62.6 13.6 %collective-permute-done.9.low_ref = bf16[256,1024]{1,0:T(8,128)(2,1)S(1)} collective-permute-done((bf16[256,1024]{1,0:T(8,128)(2,1)S(1)}, bf16[256,1024]{1,0:T(8,128)(2,1)S(1)}, u32[]{:S(2)}, u32[]{:S(2)}) %collective-permute-start.9) | collective-permute-done | bytes 524320 | tf_op jit(solution)/shard_map/ppermute | solution.py:53
  76.1 8.3 %collective-permute-done.12.refs_1_ = bf16[8,32,2048]{2,1,0:T(8,128)(2,1)S(1)} collective-permute-done((bf16[8,32,2048]{2,1,0:T(8,128)(2,1)S(1)}, bf16[8,32,2048]{2,1,0:T(8,128)(2,1)S(1)}, u32[]{:S(2)}, u32[]{:S(2)}) %collective-permute-start.12) | collective-permute-done | bytes 1048608 | tf_op jit(solution)/shard_map/ppermute | solution.py:327
  84.5 0.0 collective-permute-done.13.refs_2_
  84.5 6.2 %collective-permute-done.14.refs_4_ = bf16[8,32,2048]{2,1,0:T(8,128)(2,1)S(1)} collective-permute-done((bf16[8,32,2048]{2,1,0:T(8,128)(2,1)S(1)}, bf16[8,32,2048]{2,1,0:T(8,128)(2,1)S(1)}, u32[]{:S(2)}, u32[]{:S(2)}) %collective-permute-start.14) | collective-permute-done | bytes 1048608 | tf_op jit(solution)/shard_map/ppermute | solution.py:331
  90.6 0.0 collective-permute-done.15.refs_7_
  90.6 0.6 collective-permute-start.17
  91.2 1.2 collective-permute-start.18
  92.4 4.4 %qkv.1 = (bf16[256,1024]{1,0:T(8,128)(2,1)S(1)}, bf16[768,2048]{1,0:T(8,128)(2,1)S(1)}) custom-call(bf16[256,1024]{1,0:T(8,128)(2,1)S(1)} %collective-permute-done.9.low_ref, bf16[256,1024]{1,0:T(8,128)(2,1)S(1)} %get-tuple-element.37.own_ref, bf16[256,1024]{1,0:T(8,128)(2,1)S(1)} %collective-permute-done.10.high_ref, bf16[1024,3072]{1,0:T(8,128)(2,1)S(1)} %copy-done), custom_call_target="tpu_custom_call" | custom-call | flops 1 | bytes 1 | tf_op jit(solution)/shard_map/qkv/pallas_call | solution.py:158
  96.9 11.7 %attention.1 = (f32[256,1024]{1,0:T(8,128)S(1)}, bf16[256,1024]{1,0:T(8,128)(2,1)S(1)}) custom-call(s32[8]{0:T(128)S(1)} %stack.49.place_ref.where_ref, bf16[256,1024]{1,0:T(8,128)(2,1)S(1)} %get-tuple-element.44.query_ref, bf16[768,2048]{1,0:T(8,128)(2,1)S(1)} %get-tuple-element.45.kv_ref, s32[1,256]{1,0:T(1,128)S(1)} %bitcast.26, ...), custom_call_target="tpu_custom_call" | custom-call | flops 1 | bytes 1 | tf_op jit(solution)/shard_map/attention/pallas_call | solution.py:224
  108.6 0.0 copy-start.11
  108.6 0.3 collective-permute-start.16
  108.9 1.9 %collective-permute-done.16.other_ref = bf16[256,1024]{1,0:T(8,128)(2,1)S(1)} collective-permute-done((bf16[256,1024]{1,0:T(8,128)(2,1)S(1)}, bf16[256,1024]{1,0:T(8,128)(2,1)S(1)}, u32[]{:S(2)}, u32[]{:S(2)}) %collective-permute-start.16) | collective-permute-done | bytes 524320 | tf_op jit(solution)/shard_map/ppermute | solution.py:57
  110.8 5.8 %mlp_parts.1 = (f32[256,1024]{1,0:T(8,128)S(1)}, f32[256,1024]{1,0:T(8,128)S(1)}) custom-call(s32[8]{0:T(128)S(1)} %stack.49.place_ref.where_ref, bf16[256,1024]{1,0:T(8,128)(2,1)S(1)} %get-tuple-element.48.own_ref, bf16[256,1024]{1,0:T(8,128)(2,1)S(1)} %collective-permute-done.16.other_ref, bf16[8,32,2048]{2,1,0:T(8,128)(2,1)S(1)} %get-tuple-element.40.refs_0_, ...), custom_call_target="tpu_custom_call" | custom-call | flops 1 | bytes 1 | tf_op jit(solution)/shard_map/mlp_parts/pallas_call | solution.py:311
  116.6 0.2 collective-permute-start.19
  116.9 0.0 copy-start.8
  116.9 2.5 %collective-permute-done.19.other_ref = f32[256,1024]{1,0:T(8,128)S(1)} collective-permute-done((f32[256,1024]{1,0:T(8,128)S(1)}, f32[256,1024]{1,0:T(8,128)S(1)}, u32[]{:S(2)}, u32[]{:S(2)}) %collective-permute-start.19) | collective-permute-done | bytes 1048608 | tf_op jit(solution)/shard_map/ppermute | solution.py:57
  119.4 0.7 final_head.1
  120.1 0.2 collective-permute-start.20
  120.3 1.1 collective-permute-done.20
  121.4 2.5 %collective-permute-start.21 = (bf16[2,112,256]{2,1,0:T(8,128)(2,1)S(1)}, bf16[2,112,256]{2,1,0:T(8,128)(2,1)S(1)}, u32[]{:S(2)}, u32[]{:S(2)}) collective-permute-start(bf16[2,112,256]{2,1,0:T(8,128)(2,1)S(1)} %pad_maximum_fusion.3), channel_id=1, source_target_pairs={{0,128},{128,0},{1,129},{129,1},{2,130},{130,2},{3,131},{131,3},{4... | collective-permute-start | bytes 344072 | tf_op jit(solution)/shard_map/ppermute | solution.py:525
  123.9 4.3 %collective-permute-done.21 = bf16[2,112,256]{2,1,0:T(8,128)(2,1)S(1)} collective-permute-done((bf16[2,112,256]{2,1,0:T(8,128)(2,1)S(1)}, bf16[2,112,256]{2,1,0:T(8,128)(2,1)S(1)}, u32[]{:S(2)}, u32[]{:S(2)}) %collective-permute-start.21) | collective-permute-done | bytes 114720 | tf_op jit(solution)/shard_map/ppermute | solution.py:525
  128.3 0.1 collective-permute-start.22
  128.3 6.2 %collective-permute-start.23 = (bf16[4,112,256]{2,1,0:T(8,128)(2,1)S(1)}, bf16[4,112,256]{2,1,0:T(8,128)(2,1)S(1)}, u32[]{:S(2)}, u32[]{:S(2)}) collective-permute-start(bf16[4,112,256]{2,1,0:T(8,128)(2,1)S(1)} %pad_maximum_fusion.1.refs_1_), channel_id=1, source_target_pairs={{1,0},{2,1},{3,2},{4,3},{5,4},{6,5},{7,6},{8,7},{9,8},{10,9},{11,1... | collective-permute-start | bytes 688136 | tf_op jit(solution)/shard_map/ppermute | solution.py:53
  134.6 1.8 %decoder_tallies.1.tally_ref = bf16[768,1024]{1,0:T(8,128)(2,1)S(1)} custom-call(s32[8]{0:T(128)S(1)} %stack.49.place_ref.where_ref, s32[4,1024]{1,0:T(4,128)S(1)} %bitcast.23), custom_call_target="tpu_custom_call" | custom-call | flops 1 | bytes 1 | tf_op jit(solution)/shard_map/decoder_tallies/pallas_call | solution.py:376
  136.4 3.0 %collective-permute-done.22.refs_0_ = bf16[4,112,256]{2,1,0:T(8,128)(2,1)S(1)} collective-permute-done((bf16[4,112,256]{2,1,0:T(8,128)(2,1)S(1)}, bf16[4,112,256]{2,1,0:T(8,128)(2,1)S(1)}, u32[]{:S(2)}, u32[]{:S(2)}) %collective-permute-start.22) | collective-permute-done | bytes 229408 | tf_op jit(solution)/shard_map/ppermute | solution.py:53
  139.4 2.0 %decoder_crps.1 = f32[100,1,1024]{2,1,0:T(1,128)} custom-call(bf16[768,1024]{1,0:T(8,128)(2,1)S(1)} %decoder_tallies.1.tally_ref, bf16[218,1024]{1,0:T(8,128)(2,1)S(1)} %copy-done.2, bf16[100,1024]{1,0:T(8,128)(2,1)S(1)} %copy-done.5, bf16[4,112,256]{2,1,0:T(8,128)(2,1)S(1)} %collective-permute-done.22.refs_0_, ...), custom_call_target="tpu_custom_call" | custom-call | flops 1 | bytes 1 | tf_op jit(solution)/shard_map/decoder_crps/pallas_call | solution.py:419
  (25 shorter events, 0.1 us)
Async XLA Ops:
  0.0 22.0 %copy-start.2 = (bf16[218,1024]{1,0:T(8,128)(2,1)S(1)}, bf16[218,1024]{1,0:T(8,128)(2,1)}, u32[]{:S(2)}) copy-start(bf16[218,1024]{1,0:T(8,128)(2,1)} %state_ref.1) | copy-start | bytes 1339396
  1.0 14.1 %collective-permute-start = (bf16[32,2048]{1,0:T(8,128)(2,1)S(1)}, bf16[32,2048]{1,0:T(8,128)(2,1)S(1)}, u32[]{:S(2)}, u32[]{:S(2)}) collective-permute-start(bf16[32,2048]{1,0:T(8,128)(2,1)S(1)} %get-tuple-element.56), channel_id=1, source_target_pairs={{0,16},{8,24},{16,0},{24,8},{1,17},{9,25},{17,1},{25,9},{2,18},{10... | collective-permute-start | bytes 393224 | tf_op jit(solution)/shard_map/ppermute | solution.py:327
  4.1 17.9 %collective-permute-start.1 = (bf16[218,1024]{1,0:T(8,128)(2,1)}, bf16[218,1024]{1,0:T(8,128)(2,1)S(1)}, u32[]{:S(2)}, u32[]{:S(2)}) collective-permute-start(bf16[218,1024]{1,0:T(8,128)(2,1)} %state_ref.1), channel_id=1, source_target_pairs={{0,1},{1,2},{2,3},{3,4},{4,5},{5,6},{6,7},{7,8},{8,9},{9,10},{10,1... | collective-permute-start | bytes 1339400 | tf_op jit(solution)/shard_map/ppermute | solution.py:53
  6.0 16.0 %collective-permute-start.2 = (bf16[218,1024]{1,0:T(8,128)(2,1)}, bf16[218,1024]{1,0:T(8,128)(2,1)S(1)}, u32[]{:S(2)}, u32[]{:S(2)}) collective-permute-start(bf16[218,1024]{1,0:T(8,128)(2,1)} %state_ref.1), channel_id=1, source_target_pairs={{1,0},{2,1},{3,2},{4,3},{5,4},{6,5},{7,6},{8,7},{9,8},{10,9},{11,1... | collective-permute-start | bytes 1339400 | tf_op jit(solution)/shard_map/ppermute | solution.py:53
  10.5 0.7 copy-start.7
  11.2 0.7 copy-start.9
  11.9 25.9 %copy-start.3 = (bf16[1,256,1024]{2,1,0:T(8,128)(2,1)S(1)}, bf16[1,256,1024]{2,1,0:T(8,128)(2,1)}, u32[]{:S(2)}) copy-start(bf16[1,256,1024]{2,1,0:T(8,128)(2,1)} %param.20) | copy-start | bytes 1572868
  15.1 22.7 %copy-start.4 = (bf16[218,1024]{1,0:T(8,128)(2,1)S(1)}, bf16[218,1024]{1,0:T(8,128)(2,1)}, u32[]{:S(2)}) copy-start(bf16[218,1024]{1,0:T(8,128)(2,1)} %embed_ref.1) | copy-start | bytes 1339396
  15.1 22.7 %copy-start.6 = (f32[3,1024]{1,0:T(4,128)S(1)}, f32[3,1024]{1,0:T(4,128)}, u32[]{:S(2)}) copy-start(f32[3,1024]{1,0:T(4,128)} %gain_ref.5) | copy-start | bytes 36868
  15.1 77.3 %copy-start = (bf16[1024,3072]{1,0:T(8,128)(2,1)S(1)}, bf16[1024,3072]{1,0:T(8,128)(2,1)}, u32[]{:S(2)}) copy-start(bf16[1024,3072]{1,0:T(8,128)(2,1)} %qkv_hbm.1) | copy-start | bytes 18874372
  15.2 10.8 %collective-permute-start.3 = (bf16[2,32,2048]{2,1,0:T(8,128)(2,1)S(1)}, bf16[2,32,2048]{2,1,0:T(8,128)(2,1)S(1)}, u32[]{:S(2)}, u32[]{:S(2)}) collective-permute-start(bf16[2,32,2048]{2,1,0:T(8,128)(2,1)S(1)} %pad_maximum_fusion.refs_0_), channel_id=1, source_target_pairs={{0,1},{1,2},{2,3},{3,4},{4,5},{5,6},{6,7},{7,0},{8,9},{9,10},{10,1... | collective-permute-start | bytes 786440 | tf_op jit(solution)/shard_map/ppermute | solution.py:327
  15.3 10.7 %collective-permute-start.4 = (bf16[2,32,2048]{2,1,0:T(8,128)(2,1)S(1)}, bf16[2,32,2048]{2,1,0:T(8,128)(2,1)S(1)}, u32[]{:S(2)}, u32[]{:S(2)}) collective-permute-start(bf16[2,32,2048]{2,1,0:T(8,128)(2,1)S(1)} %pad_maximum_fusion.refs_0_), channel_id=1, source_target_pairs={{0,7},{1,0},{2,1},{3,2},{4,3},{5,4},{6,5},{7,6},{8,15},{9,8},{10,9... | collective-permute-start | bytes 786440 | tf_op jit(solution)/shard_map/ppermute | solution.py:327
  26.0 8.5 %collective-permute-start.5 = (bf16[2,32,2048]{2,1,0:T(8,128)(2,1)S(1)}, bf16[2,32,2048]{2,1,0:T(8,128)(2,1)S(1)}, u32[]{:S(2)}, u32[]{:S(2)}) collective-permute-start(bf16[2,32,2048]{2,1,0:T(8,128)(2,1)S(1)} %collective-permute-done.3.refs_7_), channel_id=1, source_target_pairs={{0,1},{1,2},{2,3},{3,4},{4,5},{5,6},{6,7},{7,0},{8,9},{9,10},{10,1... | collective-permute-start | bytes 786440 | tf_op jit(solution)/shard_map/ppermute | solution.py:327
  26.0 8.5 %collective-permute-start.7 = (bf16[2,32,2048]{2,1,0:T(8,128)(2,1)S(1)}, bf16[2,32,2048]{2,1,0:T(8,128)(2,1)S(1)}, u32[]{:S(2)}, u32[]{:S(2)}) collective-permute-start(bf16[2,32,2048]{2,1,0:T(8,128)(2,1)S(1)} %collective-permute-done.4.refs_1_), channel_id=1, source_target_pairs={{0,7},{1,0},{2,1},{3,2},{4,3},{5,4},{6,5},{7,6},{8,15},{9,8},{10,9... | collective-permute-start | bytes 786440 | tf_op jit(solution)/shard_map/ppermute | solution.py:327
  34.5 7.6 %collective-permute-start.6 = (bf16[2,32,2048]{2,1,0:T(8,128)(2,1)S(1)}, bf16[2,32,2048]{2,1,0:T(8,128)(2,1)S(1)}, u32[]{:S(2)}, u32[]{:S(2)}) collective-permute-start(bf16[2,32,2048]{2,1,0:T(8,128)(2,1)S(1)} %collective-permute-done.5.refs_6_), channel_id=1, source_target_pairs={{0,1},{1,2},{2,3},{3,4},{4,5},{5,6},{6,7},{7,0},{8,9},{9,10},{10,1... | collective-permute-start | bytes 786440 | tf_op jit(solution)/shard_map/ppermute | solution.py:327
  34.5 8.0 %collective-permute-start.8 = (bf16[2,32,2048]{2,1,0:T(8,128)(2,1)S(1)}, bf16[2,32,2048]{2,1,0:T(8,128)(2,1)S(1)}, u32[]{:S(2)}, u32[]{:S(2)}) collective-permute-start(bf16[2,32,2048]{2,1,0:T(8,128)(2,1)S(1)} %collective-permute-done.7.refs_2_), channel_id=1, source_target_pairs={{0,7},{1,0},{2,1},{3,2},{4,3},{5,4},{6,5},{7,6},{8,15},{9,8},{10,9... | collective-permute-start | bytes 786440 | tf_op jit(solution)/shard_map/ppermute | solution.py:327
  42.6 8.0 %collective-permute-start.11 = (bf16[2,32,2048]{2,1,0:T(8,128)(2,1)S(1)}, bf16[2,32,2048]{2,1,0:T(8,128)(2,1)S(1)}, u32[]{:S(2)}, u32[]{:S(2)}) collective-permute-start(bf16[2,32,2048]{2,1,0:T(8,128)(2,1)S(1)} %collective-permute-done.6.refs_5_), channel_id=1, source_target_pairs={{0,1},{1,2},{2,3},{3,4},{4,5},{5,6},{6,7},{7,0},{8,9},{9,10},{10,1... | collective-permute-start | bytes 786440 | tf_op jit(solution)/shard_map/ppermute | solution.py:327
  42.6 20.0 %collective-permute-start.10 = (bf16[256,1024]{1,0:T(8,128)(2,1)S(1)}, bf16[256,1024]{1,0:T(8,128)(2,1)S(1)}, u32[]{:S(2)}, u32[]{:S(2)}) collective-permute-start(bf16[256,1024]{1,0:T(8,128)(2,1)S(1)} %get-tuple-element.37.own_ref), channel_id=1, source_target_pairs={{1,0},{2,1},{3,2},{4,3},{5,4},{6,5},{7,6},{8,7},{9,8},{10,9},{11,1... | collective-permute-start | bytes 1572872 | tf_op jit(solution)/shard_map/ppermute | solution.py:53
  51.3 33.1 %collective-permute-start.12 = (bf16[8,32,2048]{2,1,0:T(8,128)(2,1)S(1)}, bf16[8,32,2048]{2,1,0:T(8,128)(2,1)S(1)}, u32[]{:S(2)}, u32[]{:S(2)}) collective-permute-start(bf16[8,32,2048]{2,1,0:T(8,128)(2,1)S(1)} %get-tuple-element.40.refs_0_), channel_id=1, source_target_pairs={{0,8},{8,16},{16,24},{24,0},{1,9},{9,17},{17,25},{25,1},{2,10},{10... | collective-permute-start | bytes 3145736 | tf_op jit(solution)/shard_map/ppermute | solution.py:327
  58.8 25.7 %collective-permute-start.13 = (bf16[8,32,2048]{2,1,0:T(8,128)(2,1)S(1)}, bf16[8,32,2048]{2,1,0:T(8,128)(2,1)S(1)}, u32[]{:S(2)}, u32[]{:S(2)}) collective-permute-start(bf16[8,32,2048]{2,1,0:T(8,128)(2,1)S(1)} %get-tuple-element.40.refs_0_), channel_id=1, source_target_pairs={{0,24},{8,0},{16,8},{24,16},{1,25},{9,1},{17,9},{25,17},{2,26},{10... | collective-permute-start | bytes 3145736 | tf_op jit(solution)/shard_map/ppermute | solution.py:327
  58.8 31.8 %collective-permute-start.14 = (bf16[8,32,2048]{2,1,0:T(8,128)(2,1)S(1)}, bf16[8,32,2048]{2,1,0:T(8,128)(2,1)S(1)}, u32[]{:S(2)}, u32[]{:S(2)}) collective-permute-start(bf16[8,32,2048]{2,1,0:T(8,128)(2,1)S(1)} %get-tuple-element.40.refs_0_), channel_id=1, source_target_pairs={{0,32},{32,0},{1,33},{33,1},{2,34},{34,2},{3,35},{35,3},{4,36},{36... | collective-permute-start | bytes 3145736 | tf_op jit(solution)/shard_map/ppermute | solution.py:331
  59.0 37.8 %copy-start.1 = (bf16[1024,1024]{1,0:T(8,128)(2,1)S(1)}, bf16[1024,1024]{1,0:T(8,128)(2,1)}, u32[]{:S(2)}) copy-start(bf16[1024,1024]{1,0:T(8,128)(2,1)} %out_hbm.1) | copy-start | bytes 6291460
  59.0 37.8 %copy-start.10 = (s32[256]{0:T(256)S(1)}, s32[256]{0:T(256)}, u32[]{:S(2)}) copy-start(s32[256]{0:T(256)} %param.18) | copy-start | bytes 3076
  59.0 31.6 %collective-permute-start.15 = (bf16[8,32,2048]{2,1,0:T(8,128)(2,1)S(1)}, bf16[8,32,2048]{2,1,0:T(8,128)(2,1)S(1)}, u32[]{:S(2)}, u32[]{:S(2)}) collective-permute-start(bf16[8,32,2048]{2,1,0:T(8,128)(2,1)S(1)} %get-tuple-element.41.refs_3_), channel_id=1, source_target_pairs={{0,160},{160,0},{32,128},{128,32},{1,161},{161,1},{33,129},{129,33... | collective-permute-start | bytes 3145736 | tf_op jit(solution)/shard_map/ppermute | solution.py:335
  62.6 13.6 %collective-permute-start.9 = (bf16[256,1024]{1,0:T(8,128)(2,1)S(1)}, bf16[256,1024]{1,0:T(8,128)(2,1)S(1)}, u32[]{:S(2)}, u32[]{:S(2)}) collective-permute-start(bf16[256,1024]{1,0:T(8,128)(2,1)S(1)} %get-tuple-element.37.own_ref), channel_id=1, source_target_pairs={{0,1},{1,2},{2,3},{3,4},{4,5},{5,6},{6,7},{7,8},{8,9},{9,10},{10,1... | collective-permute-start | bytes 1572872 | tf_op jit(solution)/shard_map/ppermute | solution.py:53
  90.6 20.2 %collective-permute-start.17 = (bf16[8,32,2048]{2,1,0:T(8,128)(2,1)S(1)}, bf16[8,32,2048]{2,1,0:T(8,128)(2,1)S(1)}, u32[]{:S(2)}, u32[]{:S(2)}) collective-permute-start(bf16[8,32,2048]{2,1,0:T(8,128)(2,1)S(1)} %collective-permute-done.12.refs_1_), channel_id=1, source_target_pairs={{0,32},{32,0},{1,33},{33,1},{2,34},{34,2},{3,35},{35,3},{4,36},{36... | collective-permute-start | bytes 3145736 | tf_op jit(solution)/shard_map/ppermute | solution.py:331
  91.2 19.6 %collective-permute-start.18 = (bf16[8,32,2048]{2,1,0:T(8,128)(2,1)S(1)}, bf16[8,32,2048]{2,1,0:T(8,128)(2,1)S(1)}, u32[]{:S(2)}, u32[]{:S(2)}) collective-permute-start(bf16[8,32,2048]{2,1,0:T(8,128)(2,1)S(1)} %collective-permute-done.13.refs_2_), channel_id=1, source_target_pairs={{0,160},{160,0},{32,128},{128,32},{1,161},{161,1},{33,129},{129,33... | collective-permute-start | bytes 3145736 | tf_op jit(solution)/shard_map/ppermute | solution.py:335
  108.6 8.3 %copy-start.11 = (bf16[1024,100]{0,1:T(8,128)(2,1)S(1)}, bf16[1024,100]{0,1:T(8,128)(2,1)}, u32[]{:S(2)}) copy-start(bf16[1024,100]{0,1:T(8,128)(2,1)} %param.27) | copy-start | bytes 614404
  108.6 2.2 %collective-permute-start.16 = (bf16[256,1024]{1,0:T(8,128)(2,1)S(1)}, bf16[256,1024]{1,0:T(8,128)(2,1)S(1)}, u32[]{:S(2)}, u32[]{:S(2)}) collective-permute-start(bf16[256,1024]{1,0:T(8,128)(2,1)S(1)} %get-tuple-element.48.own_ref), channel_id=1, source_target_pairs={{0,64},{64,0},{1,65},{65,1},{2,66},{66,2},{3,67},{67,3},{4,68},{68... | collective-permute-start | bytes 1572872 | tf_op jit(solution)/shard_map/ppermute | solution.py:57
  116.6 2.7 %collective-permute-start.19 = (f32[256,1024]{1,0:T(8,128)S(1)}, f32[256,1024]{1,0:T(8,128)S(1)}, u32[]{:S(2)}, u32[]{:S(2)}) collective-permute-start(f32[256,1024]{1,0:T(8,128)S(1)} %get-tuple-element.54), channel_id=1, source_target_pairs={{0,64},{64,0},{1,65},{65,1},{2,66},{66,2},{3,67},{67,3},{4,68},{68... | collective-permute-start | bytes 3145736 | tf_op jit(solution)/shard_map/ppermute | solution.py:57
  116.9 17.7 %copy-start.8 = (s32[1024,4]{0,1:T(4,128)S(1)}, s32[1024,4]{0,1:T(4,128)}, u32[]{:S(2)}) copy-start(s32[1024,4]{0,1:T(4,128)} %param.19) | copy-start | bytes 49156
  119.4 20.0 %copy-start.5 = (bf16[100,1024]{1,0:T(8,128)(2,1)S(1)}, bf16[100,1024]{1,0:T(8,128)(2,1)}, u32[]{:S(2)}) copy-start(bf16[100,1024]{1,0:T(8,128)(2,1)} %truth_ref.1) | copy-start | bytes 614404
  120.1 1.3 collective-permute-start.20
  121.4 6.8 %collective-permute-start.21 = (bf16[2,112,256]{2,1,0:T(8,128)(2,1)S(1)}, bf16[2,112,256]{2,1,0:T(8,128)(2,1)S(1)}, u32[]{:S(2)}, u32[]{:S(2)}) collective-permute-start(bf16[2,112,256]{2,1,0:T(8,128)(2,1)S(1)} %pad_maximum_fusion.3), channel_id=1, source_target_pairs={{0,128},{128,0},{1,129},{129,1},{2,130},{130,2},{3,131},{131,3},{4... | collective-permute-start | bytes 344072 | tf_op jit(solution)/shard_map/ppermute | solution.py:525
  128.3 11.1 %collective-permute-start.22 = (bf16[4,112,256]{2,1,0:T(8,128)(2,1)S(1)}, bf16[4,112,256]{2,1,0:T(8,128)(2,1)S(1)}, u32[]{:S(2)}, u32[]{:S(2)}) collective-permute-start(bf16[4,112,256]{2,1,0:T(8,128)(2,1)S(1)} %pad_maximum_fusion.1.refs_1_), channel_id=1, source_target_pairs={{0,1},{1,2},{2,3},{3,4},{4,5},{5,6},{6,7},{7,8},{8,9},{9,10},{10,1... | collective-permute-start | bytes 688136 | tf_op jit(solution)/shard_map/ppermute | solution.py:53
  128.3 11.0 %collective-permute-start.23 = (bf16[4,112,256]{2,1,0:T(8,128)(2,1)S(1)}, bf16[4,112,256]{2,1,0:T(8,128)(2,1)S(1)}, u32[]{:S(2)}, u32[]{:S(2)}) collective-permute-start(bf16[4,112,256]{2,1,0:T(8,128)(2,1)S(1)} %pad_maximum_fusion.1.refs_1_), channel_id=1, source_target_pairs={{1,0},{2,1},{3,2},{4,3},{5,4},{6,5},{7,6},{8,7},{9,8},{10,9},{11,1... | collective-permute-start | bytes 688136 | tf_op jit(solution)/shard_map/ppermute | solution.py:53
where the time goes:
time: 142 us; the launch traced here: 141 us
  waiting for transfers between devices  59.8 us (42%)
  starting transfers between devices  47.4 us (33%)
  Pallas kernels  31.4 us (22%)
  local copies, waits for them, and re-layouts  2.48 us (2%)
    ppermute x10, waiting for transfers between devices, turn(): lax.ppermute(block, axis, [(i, (i + step) % count) for i in range(count)])  23.7 us
    ppermute x10, starting transfers between devices, turn(): lax.ppermute(block, axis, [(i, (i + step) % count) for i in range(count)])  20.6 us
    ppermute x3, waiting for transfers between devices, neighbours(): lax.ppermute(block, NODE, forward)  20.1 us
    ppermute x3, starting transfers between devices, neighbours(): lax.ppermute(block, NODE, backward)  16 us
    pallas_call x1, Pallas kernels, attention(): pl.pallas_call(attention_kernel, out_shape=(jax.ShapeDtypeStruct((nodes,...  11.7 us
    ppermute x2, waiting for transfers between devices, beside(): return lax.ppermute(block, NODE[0], [(0, 1), (1, 0)])  6.17 us
    pallas_call x1, Pallas kernels, mlp_parts(): pl.pallas_call(mlp_kernel, out_shape=(jax.ShapeDtypeStruct((nodes, width)...  5.81 us
    ppermute x3, waiting for transfers between devices, other_core(): return lax.ppermute(block, 'member_core', [(0, 1), (1, 0)])  5.5 us
  transfers between devices with their start and end apart: 24, of which 14 were waited for; matrix products, arithmetic and copies ran while one was open for 0% of the time, Pallas kernels for 16%

commit v1 on v0

--- a/solution.py
+++ b/solution.py
@@ -170,11 +170,8 @@
 
 
 def attention_kernel(
-    where_ref, query_ref, kv_ref, reach_ref, start_ref, gain_ref, out_hbm,
-    mid_ref, normed_ref, cap_ref, attended_ref, out_ref, sem,
+    where_ref, query_ref, kv_ref, reach_ref, attended_ref, cap_ref,
 ):
-    copy = pltpu.make_async_copy(out_hbm, out_ref, sem)
-    copy.start()
     nodes, width = query_ref.shape
     rows = cap_ref.shape[1]
     span = cap_ref.shape[2]
@@ -197,49 +194,59 @@
             queries = query_ref[block * rows : (block + 1) * rows, columns]
             keys = kv_ref[block * rows : block * rows + span, columns]
             values = kv_ref[block * rows : block * rows + span, value_columns]
-            halves = []
-            for side in range(2):
-                mine = (lane < HEAD_DIM) if side == 0 else (lane >= HEAD_DIM)
-                chosen = jnp.where(mine, queries, jnp.zeros_like(queries))
-                scores = jnp.minimum(dot_lanes(chosen, keys), cap[...])
-                highest = jnp.max(scores, axis=-1, keepdims=True)
-                weights = jnp.exp(scores - highest)
-                total = jnp.sum(weights, axis=-1, keepdims=True)
-                blended = dot(weights.astype(BF16), values)
-                halves.append(blended * (1.0 / total))
+            nothing = jnp.zeros_like(queries)
+            chosen = jnp.concatenate(
+                [
+                    jnp.where(lane < HEAD_DIM, queries, nothing),
+                    jnp.where(lane < HEAD_DIM, nothing, queries),
+                ],
+                axis=0,
+            )
+            scores = dot_lanes(chosen, keys)
+            scores = jnp.minimum(scores.reshape(2, rows, span), cap[...][None])
+            highest = jnp.max(scores, axis=-1, keepdims=True)
+            weights = jnp.exp(scores - highest)
+            total = jnp.sum(weights, axis=-1, keepdims=True)
+            blended = dot(weights.astype(BF16).reshape(2 * rows, span), values)
+            blended = blended.reshape(2, rows, 2 * HEAD_DIM) * (1.0 / total)
             attended_ref[block * rows : (block + 1) * rows, columns] = jnp.where(
-                lane < HEAD_DIM, halves[0], halves[1]
+                lane < HEAD_DIM, blended[0], blended[1]
             ).astype(BF16)
-    copy.wait()
+
+
+def middle_kernel(start_ref, attended_ref, out_ref, gain_ref, mid_ref, normed_ref):
     middle = start_ref[...] + dot(attended_ref[...], out_ref[...])
     mid_ref[...] = middle
     normed_ref[...] = layer_norm(middle, gain_ref[1:2, :]).astype(BF16)
 
 
-def attention(where, query, kv, reach, start, norm_gains, out_weight):
+def middle_of(start, attended, out_weight, norm_gains):
+    return pl.pallas_call(
+        middle_kernel,
+        out_shape=(
+            jax.ShapeDtypeStruct(start.shape, F32),
+            jax.ShapeDtypeStruct(start.shape, BF16),
+        ),
+        compiler_params=params(24),
+        cost_estimate=SHORT,
+        name="middle",
+    )(start, attended, out_weight, norm_gains)
+
+
+def attention(where, query, kv, reach):
     nodes, width = query.shape
     rows = 128
     span = rows + 2 * BAND
     vmem = pl.BlockSpec(memory_space=pltpu.VMEM)
     return pl.pallas_call(
         attention_kernel,
-        out_shape=(
-            jax.ShapeDtypeStruct((nodes, width), F32),
-            jax.ShapeDtypeStruct((nodes, width), BF16),
-        ),
-        in_specs=[pl.BlockSpec(memory_space=pltpu.SMEM)]
-        + [vmem] * 5
-        + [pl.BlockSpec(memory_space=pl.ANY)],
-        scratch_shapes=[
-            pltpu.VMEM((nodes // rows, rows, span), F32),
-            pltpu.VMEM((nodes, width), BF16),
-            pltpu.VMEM(out_weight.shape, BF16),
-            pltpu.SemaphoreType.DMA,
-        ],
+        out_shape=jax.ShapeDtypeStruct((nodes, width), BF16),
+        in_specs=[pl.BlockSpec(memory_space=pltpu.SMEM)] + [vmem] * 3,
+        scratch_shapes=[pltpu.VMEM((nodes // rows, rows, span), F32)],
         compiler_params=params(32),
         cost_estimate=SHORT,
         name="attention",
-    )(where, query, kv, reach, start, norm_gains, out_weight)
+    )(where, query, kv, reach)
 
 
 def in_order_kernel(place_ref, *refs):
@@ -264,8 +271,8 @@
 
 
 def mlp_kernel(place_ref, own_ref, other_ref, *refs):
-    blocks = refs[:8]
-    own_out, other_out, tokens_ref, total_ref = refs[8:]
+    blocks = refs[:-4]
+    own_out, other_out, tokens_ref, total_ref = refs[-4:]
     nodes, width = own_ref.shape
     part = width // 8
     hidden = blocks[0].shape[2]
@@ -300,7 +307,7 @@
             total_ref[...] += lowered
     for block in range(8):
         columns = slice(block * part, (block + 1) * part)
-        other_out[:, at(block)] = total_ref[:nodes, columns]
+        other_out[:, at(block)] = total_ref[:nodes, columns].astype(BF16)
         own_out[:, at(block)] = total_ref[nodes:, columns]
 
 
@@ -310,7 +317,10 @@
     vmem = pl.BlockSpec(memory_space=pltpu.VMEM)
     return pl.pallas_call(
         mlp_kernel,
-        out_shape=(jax.ShapeDtypeStruct((nodes, width), F32),) * 2,
+        out_shape=(
+            jax.ShapeDtypeStruct((nodes, width), F32),
+            jax.ShapeDtypeStruct((nodes, width), BF16),
+        ),
         in_specs=[pl.BlockSpec(memory_space=pltpu.SMEM)] + [vmem] * (2 + len(blocks)),
         scratch_shapes=[
             pltpu.VMEM((2 * nodes, width), BF16),
@@ -336,7 +346,7 @@
 
 
 def head_kernel(mid_ref, own_ref, other_ref, gain_ref, head_ref, out_ref):
-    ending = mid_ref[...] + (own_ref[...] + other_ref[...])
+    ending = mid_ref[...] + (own_ref[...] + other_ref[...].astype(F32))
     final = layer_norm(ending, gain_ref[2:3, :]).astype(BF16)
     out_ref[...] = dot_lanes(head_ref[...], final).astype(BF16)
 
@@ -494,25 +504,26 @@
     after = turn(column, NODE[1], -1)
     other_column = beside(column)
     other_far = across(far)
-    normed_low, normed_high, before, after, other_column, other_far = tie(
-        (normed_low, normed_high, before, after, other_column, other_far)
-    )
-
-    other_before = beside(before)
-    other_after = across(after)
     query, kv = qkv(normed_low, normed, normed_high, qkv_weight)
     decoder_near = decoder_tallies(place, decoder_slots.T, 3 * node_dev)
-    middle, normed_mid = attention(
-        place, query, kv, node_reach[None, :], start, norm_gains, out_weight
-    )
+    query, kv, decoder_near, before, after, other_column, other_far = tie(
+        (query, kv, decoder_near, before, after, other_column, other_far)
+    )
+
+    half = column.shape[0] // 2
+    other_before = (beside(before[:half]), turn(other_column[half:], NODE[1], 1))
+    other_after = (across(after[:half]), turn(other_column[half:], NODE[1], -1))
+    attended = attention(place, query, kv, node_reach[None, :])
+    attended, other_before, other_after = tie((attended, other_before, other_after))
+    middle, normed_mid = middle_of(start, attended, out_weight, norm_gains)
     shards = (
         column,
         before,
         after,
         far,
         other_column,
-        other_before,
-        other_after,
+        *other_before,
+        *other_after,
         other_far,
     )
 

time: 142 us -> 136 us (0.958)
  waiting for transfers between devices: 59.8 us -> 52.6 us
  starting transfers between devices: 47.4 us -> 52.3 us
  Pallas kernels: 31.4 us -> 27.8 us
    ppermute x3, waiting for transfers between devices: 20.1 us -> 8.52 us  [neighbours(): lax.ppermute(block, NODE, forward)]
    ppermute x3, waiting for transfers between devices: 0.01 us -> 6.61 us  [neighbours(): lax.ppermute(block, NODE, backward)]
    ppermute x2, waiting for transfers between devices: 6.17 us -> 0.6 us  [beside(): return lax.ppermute(block, NODE[0], [(0, 1), (1, 0)])]
    pallas_call x1 -> x2, Pallas kernels: 11.7 us -> 8.18 us  [the longest x1 7.2 us: attention(): pl.pallas_call(attention_kernel, out_shape=jax.ShapeDtypeStruct((nodes, w...]
    ppermute x10 -> x12, waiting for transfers between devices: 23.7 us -> 26.5 us  [turn(): lax.ppermute(block, axis, [(i, (i + step) % count) for i in range(count)])]
    ppermute x10 -> x12, starting transfers between devices: 20.6 us -> 22.9 us  [turn(): lax.ppermute(block, axis, [(i, (i + step) % count) for i in range(count)])]
    ppermute x3, starting transfers between devices: 2 us -> 4.02 us  [neighbours(): lax.ppermute(block, NODE, forward)]
  transfers between devices with their start and end apart: 24 -> 26, of which waited for: 14 -> 15; matrix products, arithmetic and copies ran while one was open for 0% -> 0% of each run, Pallas kernels for 16% -> 14%
where the time goes in v1:
time: 136 us
  waiting for transfers between devices  52.6 us (39%)
  starting transfers between devices  52.3 us (38%)
  Pallas kernels  27.8 us (20%)
  local copies, waits for them, and re-layouts  2.6 us (2%)
    ppermute x12, waiting for transfers between devices, turn(): lax.ppermute(block, axis, [(i, (i + step) % count) for i in range(count)])  26.5 us
    ppermute x12, starting transfers between devices, turn(): lax.ppermute(block, axis, [(i, (i + step) % count) for i in range(count)])  22.9 us
    ppermute x3, starting transfers between devices, neighbours(): lax.ppermute(block, NODE, backward)  16.2 us
    ppermute x3, waiting for transfers between devices, neighbours(): lax.ppermute(block, NODE, forward)  8.52 us
    pallas_call x1, Pallas kernels, attention(): pl.pallas_call(attention_kernel, out_shape=jax.ShapeDtypeStruct((nodes, w...  7.2 us
    ppermute x3, waiting for transfers between devices, neighbours(): lax.ppermute(block, NODE, backward)  6.61 us
    pallas_call x1, Pallas kernels, mlp_parts(): pl.pallas_call(mlp_kernel, out_shape=(jax.ShapeDtypeStruct((nodes, width)...  5.79 us
    ppermute x3, waiting for transfers between devices, other_core(): return lax.ppermute(block, 'member_core', [(0, 1), (1, 0)])  4.75 us
  transfers between devices with their start and end apart: 26, of which 15 were waited for; matrix products, arithmetic and copies ran while one was open for 0% of the time, Pallas kernels for 14%

profile of v1, /device:TPU:8, one launch (start us, length us, event | category | flops | bytes accessed | tf_op | source)
XLA Modules:
  0.0 135.6 jit_solution(2695389529140216202)
XLA Ops:
  0.0 0.9 constant_dynamic-slice_fusion
  1.0 3.1 %collective-permute-start = (bf16[32,2048]{1,0:T(8,128)(2,1)S(1)}, bf16[32,2048]{1,0:T(8,128)(2,1)S(1)}, u32[]{:S(2)}, u32[]{:S(2)}) collective-permute-start(bf16[32,2048]{1,0:T(8,128)(2,1)S(1)} %get-tuple-element.68), channel_id=1, source_target_pairs={{0,16},{8,24},{16,0},{24,8},{1,17},{9,25},{17,1},{25,9},{2,18},{10... | collective-permute-start | bytes 393224 | tf_op jit(solution)/shard_map/ppermute | solution.py:337
  4.1 1.9 %collective-permute-start.1 = (bf16[218,1024]{1,0:T(8,128)(2,1)}, bf16[218,1024]{1,0:T(8,128)(2,1)S(1)}, u32[]{:S(2)}, u32[]{:S(2)}) collective-permute-start(bf16[218,1024]{1,0:T(8,128)(2,1)} %state_ref.1), channel_id=1, source_target_pairs={{0,1},{1,2},{2,3},{3,4},{4,5},{5,6},{6,7},{7,8},{8,9},{9,10},{10,1... | collective-permute-start | bytes 1339400 | tf_op jit(solution)/shard_map/ppermute | solution.py:53
  6.0 4.4 %collective-permute-start.2 = (bf16[218,1024]{1,0:T(8,128)(2,1)}, bf16[218,1024]{1,0:T(8,128)(2,1)S(1)}, u32[]{:S(2)}, u32[]{:S(2)}) collective-permute-start(bf16[218,1024]{1,0:T(8,128)(2,1)} %state_ref.1), channel_id=1, source_target_pairs={{1,0},{2,1},{3,2},{4,3},{5,4},{6,5},{7,6},{8,7},{9,8},{10,9},{11,1... | collective-permute-start | bytes 1339400 | tf_op jit(solution)/shard_map/ppermute | solution.py:53
  10.4 0.1 stack.49.place_ref.where_ref
  10.5 0.7 copy-done.7
  11.2 0.7 copy-done.9
  11.9 3.2 %encoder_tallies.1.tally_ref = bf16[3072,256]{1,0:T(8,128)(2,1)S(1)} custom-call(s32[8]{0:T(128)S(1)} %stack.49.place_ref.where_ref, s32[16,256]{1,0:T(8,128)S(1)} %bitcast.22, s32[1,256]{1,0:T(1,128)S(1)} %bitcast.24), custom_call_target="tpu_custom_call" | custom-call | flops 1 | bytes 1 | tf_op jit(solution)/shard_map/encoder_tallies/pallas_call | solution.py:88
  15.1 0.0 copy-start.3
  15.1 0.0 copy-start.4
  15.1 0.0 copy-start.6
  15.1 0.0 collective-permute-done
  15.2 0.1 collective-permute-start.3
  15.3 3.2 %collective-permute-start.4 = (bf16[2,32,2048]{2,1,0:T(8,128)(2,1)S(1)}, bf16[2,32,2048]{2,1,0:T(8,128)(2,1)S(1)}, u32[]{:S(2)}, u32[]{:S(2)}) collective-permute-start(bf16[2,32,2048]{2,1,0:T(8,128)(2,1)S(1)} %pad_maximum_fusion.refs_0_), channel_id=1, source_target_pairs={{0,7},{1,0},{2,1},{3,2},{4,3},{5,4},{6,5},{7,6},{8,15},{9,8},{10,9... | collective-permute-start | bytes 786440 | tf_op jit(solution)/shard_map/ppermute | solution.py:337
  18.5 3.5 %collective-permute-done.1.low_ref = bf16[218,1024]{1,0:T(8,128)(2,1)S(1)} collective-permute-done((bf16[218,1024]{1,0:T(8,128)(2,1)}, bf16[218,1024]{1,0:T(8,128)(2,1)S(1)}, u32[]{:S(2)}, u32[]{:S(2)}) %collective-permute-start.1) | collective-permute-done | bytes 446496 | tf_op jit(solution)/shard_map/ppermute | solution.py:53
  22.0 0.0 copy-start
  22.0 0.5 pooled.1.pooled_ref
  22.6 3.4 %collective-permute-done.3.refs_7_ = bf16[2,32,2048]{2,1,0:T(8,128)(2,1)S(1)} collective-permute-done((bf16[2,32,2048]{2,1,0:T(8,128)(2,1)S(1)}, bf16[2,32,2048]{2,1,0:T(8,128)(2,1)S(1)}, u32[]{:S(2)}, u32[]{:S(2)}) %collective-permute-start.3) | collective-permute-done | bytes 262176 | tf_op jit(solution)/shard_map/ppermute | solution.py:337
  26.0 0.0 collective-permute-done.4.refs_1_
  26.0 0.0 collective-permute-start.5
  26.0 3.4 %collective-permute-start.7 = (bf16[2,32,2048]{2,1,0:T(8,128)(2,1)S(1)}, bf16[2,32,2048]{2,1,0:T(8,128)(2,1)S(1)}, u32[]{:S(2)}, u32[]{:S(2)}) collective-permute-start(bf16[2,32,2048]{2,1,0:T(8,128)(2,1)S(1)} %collective-permute-done.4.refs_1_), channel_id=1, source_target_pairs={{0,7},{1,0},{2,1},{3,2},{4,3},{5,4},{6,5},{7,6},{8,15},{9,8},{10,9... | collective-permute-start | bytes 786440 | tf_op jit(solution)/shard_map/ppermute | solution.py:337
  29.4 5.1 %collective-permute-done.5.refs_6_ = bf16[2,32,2048]{2,1,0:T(8,128)(2,1)S(1)} collective-permute-done((bf16[2,32,2048]{2,1,0:T(8,128)(2,1)S(1)}, bf16[2,32,2048]{2,1,0:T(8,128)(2,1)S(1)}, u32[]{:S(2)}, u32[]{:S(2)}) %collective-permute-start.5) | collective-permute-done | bytes 262176 | tf_op jit(solution)/shard_map/ppermute | solution.py:337
  34.5 3.2 %collective-permute-start.8 = (bf16[2,32,2048]{2,1,0:T(8,128)(2,1)S(1)}, bf16[2,32,2048]{2,1,0:T(8,128)(2,1)S(1)}, u32[]{:S(2)}, u32[]{:S(2)}) collective-permute-start(bf16[2,32,2048]{2,1,0:T(8,128)(2,1)S(1)} %collective-permute-done.7.refs_2_), channel_id=1, source_target_pairs={{0,7},{1,0},{2,1},{3,2},{4,3},{5,4},{6,5},{7,6},{8,15},{9,8},{10,9... | collective-permute-start | bytes 786440 | tf_op jit(solution)/shard_map/ppermute | solution.py:337
  37.8 0.6 embed.1
  38.4 3.7 %collective-permute-done.6.refs_5_ = bf16[2,32,2048]{2,1,0:T(8,128)(2,1)S(1)} collective-permute-done((bf16[2,32,2048]{2,1,0:T(8,128)(2,1)S(1)}, bf16[2,32,2048]{2,1,0:T(8,128)(2,1)S(1)}, u32[]{:S(2)}, u32[]{:S(2)}) %collective-permute-start.6) | collective-permute-done | bytes 262176 | tf_op jit(solution)/shard_map/ppermute | solution.py:337
  42.1 0.5 collective-permute-start.11
  42.6 2.0 %collective-permute-start.9 = (bf16[256,1024]{1,0:T(8,128)(2,1)S(1)}, bf16[256,1024]{1,0:T(8,128)(2,1)S(1)}, u32[]{:S(2)}, u32[]{:S(2)}) collective-permute-start(bf16[256,1024]{1,0:T(8,128)(2,1)S(1)} %get-tuple-element.43.own_ref), channel_id=1, source_target_pairs={{0,1},{1,2},{2,3},{3,4},{4,5},{5,6},{6,7},{7,8},{8,9},{9,10},{10,1... | collective-permute-start | bytes 1572872 | tf_op jit(solution)/shard_map/ppermute | solution.py:53
  44.6 7.9 %collective-permute-done.11.refs_4_ = bf16[2,32,2048]{2,1,0:T(8,128)(2,1)S(1)} collective-permute-done((bf16[2,32,2048]{2,1,0:T(8,128)(2,1)S(1)}, bf16[2,32,2048]{2,1,0:T(8,128)(2,1)S(1)}, u32[]{:S(2)}, u32[]{:S(2)}) %collective-permute-start.11) | collective-permute-done | bytes 262176 | tf_op jit(solution)/shard_map/ppermute | solution.py:337
  52.6 0.7 shards_in_order.1
  53.3 6.0 %collective-permute-start.12 = (bf16[8,32,2048]{2,1,0:T(8,128)(2,1)S(1)}, bf16[8,32,2048]{2,1,0:T(8,128)(2,1)S(1)}, u32[]{:S(2)}, u32[]{:S(2)}) collective-permute-start(bf16[8,32,2048]{2,1,0:T(8,128)(2,1)S(1)} %get-tuple-element.48.refs_0_), channel_id=1, source_target_pairs={{0,8},{8,16},{16,24},{24,0},{1,9},{9,17},{17,25},{25,1},{2,10},{10... | collective-permute-start | bytes 3145736 | tf_op jit(solution)/shard_map/ppermute | solution.py:337
  59.3 0.4 collective-permute-start.14
  59.7 2.4 %collective-permute-start.15 = (bf16[8,32,2048]{2,1,0:T(8,128)(2,1)S(1)}, bf16[8,32,2048]{2,1,0:T(8,128)(2,1)S(1)}, u32[]{:S(2)}, u32[]{:S(2)}) collective-permute-start(bf16[8,32,2048]{2,1,0:T(8,128)(2,1)S(1)} %get-tuple-element.49.refs_3_), channel_id=1, source_target_pairs={{0,160},{160,0},{32,128},{128,32},{1,161},{161,1},{33,129},{129,33... | collective-permute-start | bytes 3145736 | tf_op jit(solution)/shard_map/ppermute | solution.py:345
  62.2 0.8 collective-permute-start.10
  62.9 1.8 %decoder_tallies.1.tally_ref = bf16[768,1024]{1,0:T(8,128)(2,1)S(1)} custom-call(s32[8]{0:T(128)S(1)} %stack.49.place_ref.where_ref, s32[4,1024]{1,0:T(4,128)S(1)} %bitcast.23), custom_call_target="tpu_custom_call" | custom-call | flops 1 | bytes 1 | tf_op jit(solution)/shard_map/decoder_tallies/pallas_call | solution.py:386
  64.7 6.6 %collective-permute-done.10.high_ref = bf16[256,1024]{1,0:T(8,128)(2,1)S(1)} collective-permute-done((bf16[256,1024]{1,0:T(8,128)(2,1)S(1)}, bf16[256,1024]{1,0:T(8,128)(2,1)S(1)}, u32[]{:S(2)}, u32[]{:S(2)}) %collective-permute-start.10) | collective-permute-done | bytes 524320 | tf_op jit(solution)/shard_map/ppermute | solution.py:53
  71.3 4.4 %qkv.1 = (bf16[256,1024]{1,0:T(8,128)(2,1)S(1)}, bf16[768,2048]{1,0:T(8,128)(2,1)S(1)}) custom-call(bf16[256,1024]{1,0:T(8,128)(2,1)S(1)} %collective-permute-done.9.low_ref, bf16[256,1024]{1,0:T(8,128)(2,1)S(1)} %get-tuple-element.43.own_ref, bf16[256,1024]{1,0:T(8,128)(2,1)S(1)} %collective-permute-done.10.high_ref, bf16[1024,3072]{1,0:T(8,128)(2,1)S(1)} %copy-done), custom_call_target="tpu_custom_call" | custom-call | flops 1 | bytes 1 | tf_op jit(solution)/shard_map/qkv/pallas_call | solution.py:158
  75.8 0.0 copy-start.11
  75.8 4.9 %collective-permute-done.12.refs_1_ = bf16[8,32,2048]{2,1,0:T(8,128)(2,1)S(1)} collective-permute-done((bf16[8,32,2048]{2,1,0:T(8,128)(2,1)S(1)}, bf16[8,32,2048]{2,1,0:T(8,128)(2,1)S(1)}, u32[]{:S(2)}, u32[]{:S(2)}) %collective-permute-start.12) | collective-permute-done | bytes 1048608 | tf_op jit(solution)/shard_map/ppermute | solution.py:337
  80.7 0.6 collective-permute-done.14.refs_4_
  81.3 1.1 collective-permute-start.16
  82.5 2.0 %collective-permute-start.17 = (bf16[4,32,2048]{2,1,0:T(8,128)(2,1)S(1)}, bf16[4,32,2048]{2,1,0:T(8,128)(2,1)S(1)}, u32[]{:S(2)}, u32[]{:S(2)}) collective-permute-start(bf16[4,32,2048]{2,1,0:T(8,128)(2,1)S(1)} %slice.11), channel_id=1, source_target_pairs={{0,8},{8,16},{16,24},{24,0},{1,9},{9,17},{17,25},{25,1},{2,10},{10... | collective-permute-start | bytes 1572872 | tf_op jit(solution)/shard_map/ppermute | solution.py:337
  84.5 2.1 %collective-permute-start.18 = (bf16[4,32,2048]{2,1,0:T(8,128)(2,1)S(1)}, bf16[4,32,2048]{2,1,0:T(8,128)(2,1)S(1)}, u32[]{:S(2)}, u32[]{:S(2)}) collective-permute-start(bf16[4,32,2048]{2,1,0:T(8,128)(2,1)S(1)} %slice.12), channel_id=1, source_target_pairs={{0,160},{160,0},{32,128},{128,32},{1,161},{161,1},{33,129},{129,33... | collective-permute-start | bytes 1572872 | tf_op jit(solution)/shard_map/ppermute | solution.py:345
  86.6 1.3 collective-permute-start.19
  87.9 7.2 %attention.1.attended_ref = bf16[256,1024]{1,0:T(8,128)(2,1)S(1)} custom-call(s32[8]{0:T(128)S(1)} %stack.49.place_ref.where_ref, bf16[256,1024]{1,0:T(8,128)(2,1)S(1)} %get-tuple-element.52.query_ref, bf16[768,2048]{1,0:T(8,128)(2,1)S(1)} %get-tuple-element.53.kv_ref, s32[1,256]{1,0:T(1,128)S(1)} %bitcast.26), custom_call_target="tpu_custom_call" | custom-call | flops 1 | bytes 1 | tf_op jit(solution)/shard_map/attention/pallas_call | solution.py:241
  95.1 0.0 collective-permute-done.17.refs_6_
  95.2 1.1 collective-permute-done.18.refs_7_
  96.3 1.3 collective-permute-done.19.refs_8_
  97.6 1.0 middle.1
  98.6 0.0 copy-start.12
  98.6 0.1 collective-permute-start.20
  98.7 1.9 %collective-permute-done.20.other_ref = bf16[256,1024]{1,0:T(8,128)(2,1)S(1)} collective-permute-done((bf16[256,1024]{1,0:T(8,128)(2,1)S(1)}, bf16[256,1024]{1,0:T(8,128)(2,1)S(1)}, u32[]{:S(2)}, u32[]{:S(2)}) %collective-permute-start.20) | collective-permute-done | bytes 524320 | tf_op jit(solution)/shard_map/ppermute | solution.py:57
  100.6 5.8 %mlp_parts.1 = (f32[256,1024]{1,0:T(8,128)S(1)}, bf16[256,1024]{1,0:T(8,128)(2,1)S(1)}) custom-call(s32[8]{0:T(128)S(1)} %stack.49.place_ref.where_ref, bf16[256,1024]{1,0:T(8,128)(2,1)S(1)} %get-tuple-element.59.own_ref, bf16[256,1024]{1,0:T(8,128)(2,1)S(1)} %collective-permute-done.20.other_ref, bf16[8,32,2048]{2,1,0:T(8,128)(2,1)S(1)} %get-tuple-element.48.refs_0_, ...), custom_call_target="tpu_custom_call" | custom-call | flops 1 | bytes 1 | tf_op jit(solution)/shard_map/mlp_parts/pallas_call | solution.py:318
  106.4 0.0 copy-start.5
  106.4 0.5 collective-permute-start.21
  106.9 1.7 %collective-permute-done.21.other_ref = bf16[256,1024]{1,0:T(8,128)(2,1)S(1)} collective-permute-done((bf16[256,1024]{1,0:T(8,128)(2,1)S(1)}, bf16[256,1024]{1,0:T(8,128)(2,1)S(1)}, u32[]{:S(2)}, u32[]{:S(2)}) %collective-permute-start.21) | collective-permute-done | bytes 524320 | tf_op jit(solution)/shard_map/ppermute | solution.py:57
  108.6 0.6 final_head.1
  109.3 0.2 collective-permute-start.22
  109.5 1.1 collective-permute-done.22
  110.6 2.3 %collective-permute-start.23 = (bf16[2,112,256]{2,1,0:T(8,128)(2,1)S(1)}, bf16[2,112,256]{2,1,0:T(8,128)(2,1)S(1)}, u32[]{:S(2)}, u32[]{:S(2)}) collective-permute-start(bf16[2,112,256]{2,1,0:T(8,128)(2,1)S(1)} %pad_maximum_fusion.3), channel_id=1, source_target_pairs={{0,128},{128,0},{1,129},{129,1},{2,130},{130,2},{3,131},{131,3},{4... | collective-permute-start | bytes 344072 | tf_op jit(solution)/shard_map/ppermute | solution.py:536
  112.9 4.5 %collective-permute-done.23 = bf16[2,112,256]{2,1,0:T(8,128)(2,1)S(1)} collective-permute-done((bf16[2,112,256]{2,1,0:T(8,128)(2,1)S(1)}, bf16[2,112,256]{2,1,0:T(8,128)(2,1)S(1)}, u32[]{:S(2)}, u32[]{:S(2)}) %collective-permute-start.23) | collective-permute-done | bytes 114720 | tf_op jit(solution)/shard_map/ppermute | solution.py:536
  117.4 0.1 collective-permute-start.24
  117.5 11.0 %collective-permute-start.25 = (bf16[4,112,256]{2,1,0:T(8,128)(2,1)S(1)}, bf16[4,112,256]{2,1,0:T(8,128)(2,1)S(1)}, u32[]{:S(2)}, u32[]{:S(2)}) collective-permute-start(bf16[4,112,256]{2,1,0:T(8,128)(2,1)S(1)} %pad_maximum_fusion.1.refs_1_), channel_id=1, source_target_pairs={{1,0},{2,1},{3,2},{4,3},{5,4},{6,5},{7,6},{8,7},{9,8},{10,9},{11,1... | collective-permute-start | bytes 688136 | tf_op jit(solution)/shard_map/ppermute | solution.py:53
  128.6 5.0 %collective-permute-done.24.refs_0_ = bf16[4,112,256]{2,1,0:T(8,128)(2,1)S(1)} collective-permute-done((bf16[4,112,256]{2,1,0:T(8,128)(2,1)S(1)}, bf16[4,112,256]{2,1,0:T(8,128)(2,1)S(1)}, u32[]{:S(2)}, u32[]{:S(2)}) %collective-permute-start.24) | collective-permute-done | bytes 229408 | tf_op jit(solution)/shard_map/ppermute | solution.py:53
  133.6 2.0 %decoder_crps.1 = f32[100,1,1024]{2,1,0:T(1,128)} custom-call(bf16[768,1024]{1,0:T(8,128)(2,1)S(1)} %decoder_tallies.1.tally_ref, bf16[218,1024]{1,0:T(8,128)(2,1)S(1)} %copy-done.2, bf16[100,1024]{1,0:T(8,128)(2,1)S(1)} %copy-done.5, bf16[4,112,256]{2,1,0:T(8,128)(2,1)S(1)} %collective-permute-done.24.refs_0_, ...), custom_call_target="tpu_custom_call" | custom-call | flops 1 | bytes 1 | tf_op jit(solution)/shard_map/decoder_crps/pallas_call | solution.py:429
  (35 shorter events, 0.3 us)
Async XLA Ops:
  0.0 22.0 %copy-start.2 = (bf16[218,1024]{1,0:T(8,128)(2,1)S(1)}, bf16[218,1024]{1,0:T(8,128)(2,1)}, u32[]{:S(2)}) copy-start(bf16[218,1024]{1,0:T(8,128)(2,1)} %state_ref.1) | copy-start | bytes 1339396
  0.0 22.0 %copy-start.10 = (s32[256]{0:T(256)S(1)}, s32[256]{0:T(256)}, u32[]{:S(2)}) copy-start(s32[256]{0:T(256)} %param.17) | copy-start | bytes 3076
  1.0 14.2 %collective-permute-start = (bf16[32,2048]{1,0:T(8,128)(2,1)S(1)}, bf16[32,2048]{1,0:T(8,128)(2,1)S(1)}, u32[]{:S(2)}, u32[]{:S(2)}) collective-permute-start(bf16[32,2048]{1,0:T(8,128)(2,1)S(1)} %get-tuple-element.68), channel_id=1, source_target_pairs={{0,16},{8,24},{16,0},{24,8},{1,17},{9,25},{17,1},{25,9},{2,18},{10... | collective-permute-start | bytes 393224 | tf_op jit(solution)/shard_map/ppermute | solution.py:337
  4.1 17.9 %collective-permute-start.1 = (bf16[218,1024]{1,0:T(8,128)(2,1)}, bf16[218,1024]{1,0:T(8,128)(2,1)S(1)}, u32[]{:S(2)}, u32[]{:S(2)}) collective-permute-start(bf16[218,1024]{1,0:T(8,128)(2,1)} %state_ref.1), channel_id=1, source_target_pairs={{0,1},{1,2},{2,3},{3,4},{4,5},{5,6},{6,7},{7,8},{8,9},{9,10},{10,1... | collective-permute-start | bytes 1339400 | tf_op jit(solution)/shard_map/ppermute | solution.py:53
  6.0 16.0 %collective-permute-start.2 = (bf16[218,1024]{1,0:T(8,128)(2,1)}, bf16[218,1024]{1,0:T(8,128)(2,1)S(1)}, u32[]{:S(2)}, u32[]{:S(2)}) collective-permute-start(bf16[218,1024]{1,0:T(8,128)(2,1)} %state_ref.1), channel_id=1, source_target_pairs={{1,0},{2,1},{3,2},{4,3},{5,4},{6,5},{7,6},{8,7},{9,8},{10,9},{11,1... | collective-permute-start | bytes 1339400 | tf_op jit(solution)/shard_map/ppermute | solution.py:53
  10.5 0.7 copy-start.7
  11.2 0.7 copy-start.9
  15.1 22.7 %copy-start.3 = (bf16[1,256,1024]{2,1,0:T(8,128)(2,1)S(1)}, bf16[1,256,1024]{2,1,0:T(8,128)(2,1)}, u32[]{:S(2)}) copy-start(bf16[1,256,1024]{2,1,0:T(8,128)(2,1)} %param.20) | copy-start | bytes 1572868
  15.1 22.7 %copy-start.4 = (bf16[218,1024]{1,0:T(8,128)(2,1)S(1)}, bf16[218,1024]{1,0:T(8,128)(2,1)}, u32[]{:S(2)}) copy-start(bf16[218,1024]{1,0:T(8,128)(2,1)} %embed_ref.1) | copy-start | bytes 1339396
  15.1 22.7 %copy-start.6 = (f32[3,1024]{1,0:T(4,128)S(1)}, f32[3,1024]{1,0:T(4,128)}, u32[]{:S(2)}) copy-start(f32[3,1024]{1,0:T(4,128)} %gain_ref.5) | copy-start | bytes 36868
  15.2 10.8 %collective-permute-start.3 = (bf16[2,32,2048]{2,1,0:T(8,128)(2,1)S(1)}, bf16[2,32,2048]{2,1,0:T(8,128)(2,1)S(1)}, u32[]{:S(2)}, u32[]{:S(2)}) collective-permute-start(bf16[2,32,2048]{2,1,0:T(8,128)(2,1)S(1)} %pad_maximum_fusion.refs_0_), channel_id=1, source_target_pairs={{0,1},{1,2},{2,3},{3,4},{4,5},{5,6},{6,7},{7,0},{8,9},{9,10},{10,1... | collective-permute-start | bytes 786440 | tf_op jit(solution)/shard_map/ppermute | solution.py:337
  15.3 10.7 %collective-permute-start.4 = (bf16[2,32,2048]{2,1,0:T(8,128)(2,1)S(1)}, bf16[2,32,2048]{2,1,0:T(8,128)(2,1)S(1)}, u32[]{:S(2)}, u32[]{:S(2)}) collective-permute-start(bf16[2,32,2048]{2,1,0:T(8,128)(2,1)S(1)} %pad_maximum_fusion.refs_0_), channel_id=1, source_target_pairs={{0,7},{1,0},{2,1},{3,2},{4,3},{5,4},{6,5},{7,6},{8,15},{9,8},{10,9... | collective-permute-start | bytes 786440 | tf_op jit(solution)/shard_map/ppermute | solution.py:337
  22.0 40.9 %copy-start.8 = (s32[1024,4]{0,1:T(4,128)S(1)}, s32[1024,4]{0,1:T(4,128)}, u32[]{:S(2)}) copy-start(s32[1024,4]{0,1:T(4,128)} %param.19) | copy-start | bytes 49156
  22.0 49.3 %copy-start = (bf16[1024,3072]{1,0:T(8,128)(2,1)S(1)}, bf16[1024,3072]{1,0:T(8,128)(2,1)}, u32[]{:S(2)}) copy-start(bf16[1024,3072]{1,0:T(8,128)(2,1)} %qkv_hbm.1) | copy-start | bytes 18874372
  26.0 8.5 %collective-permute-start.5 = (bf16[2,32,2048]{2,1,0:T(8,128)(2,1)S(1)}, bf16[2,32,2048]{2,1,0:T(8,128)(2,1)S(1)}, u32[]{:S(2)}, u32[]{:S(2)}) collective-permute-start(bf16[2,32,2048]{2,1,0:T(8,128)(2,1)S(1)} %collective-permute-done.3.refs_7_), channel_id=1, source_target_pairs={{0,1},{1,2},{2,3},{3,4},{4,5},{5,6},{6,7},{7,0},{8,9},{9,10},{10,1... | collective-permute-start | bytes 786440 | tf_op jit(solution)/shard_map/ppermute | solution.py:337
  26.0 8.5 %collective-permute-start.7 = (bf16[2,32,2048]{2,1,0:T(8,128)(2,1)S(1)}, bf16[2,32,2048]{2,1,0:T(8,128)(2,1)S(1)}, u32[]{:S(2)}, u32[]{:S(2)}) collective-permute-start(bf16[2,32,2048]{2,1,0:T(8,128)(2,1)S(1)} %collective-permute-done.4.refs_1_), channel_id=1, source_target_pairs={{0,7},{1,0},{2,1},{3,2},{4,3},{5,4},{6,5},{7,6},{8,15},{9,8},{10,9... | collective-permute-start | bytes 786440 | tf_op jit(solution)/shard_map/ppermute | solution.py:337
  34.5 7.6 %collective-permute-start.6 = (bf16[2,32,2048]{2,1,0:T(8,128)(2,1)S(1)}, bf16[2,32,2048]{2,1,0:T(8,128)(2,1)S(1)}, u32[]{:S(2)}, u32[]{:S(2)}) collective-permute-start(bf16[2,32,2048]{2,1,0:T(8,128)(2,1)S(1)} %collective-permute-done.5.refs_6_), channel_id=1, source_target_pairs={{0,1},{1,2},{2,3},{3,4},{4,5},{5,6},{6,7},{7,0},{8,9},{9,10},{10,1... | collective-permute-start | bytes 786440 | tf_op jit(solution)/shard_map/ppermute | solution.py:337
  34.5 7.6 %collective-permute-start.8 = (bf16[2,32,2048]{2,1,0:T(8,128)(2,1)S(1)}, bf16[2,32,2048]{2,1,0:T(8,128)(2,1)S(1)}, u32[]{:S(2)}, u32[]{:S(2)}) collective-permute-start(bf16[2,32,2048]{2,1,0:T(8,128)(2,1)S(1)} %collective-permute-done.7.refs_2_), channel_id=1, source_target_pairs={{0,7},{1,0},{2,1},{3,2},{4,3},{5,4},{6,5},{7,6},{8,15},{9,8},{10,9... | collective-permute-start | bytes 786440 | tf_op jit(solution)/shard_map/ppermute | solution.py:337
  42.1 10.5 %collective-permute-start.11 = (bf16[2,32,2048]{2,1,0:T(8,128)(2,1)S(1)}, bf16[2,32,2048]{2,1,0:T(8,128)(2,1)S(1)}, u32[]{:S(2)}, u32[]{:S(2)}) collective-permute-start(bf16[2,32,2048]{2,1,0:T(8,128)(2,1)S(1)} %collective-permute-done.6.refs_5_), channel_id=1, source_target_pairs={{0,1},{1,2},{2,3},{3,4},{4,5},{5,6},{6,7},{7,0},{8,9},{9,10},{10,1... | collective-permute-start | bytes 786440 | tf_op jit(solution)/shard_map/ppermute | solution.py:337
  42.6 19.5 %collective-permute-start.9 = (bf16[256,1024]{1,0:T(8,128)(2,1)S(1)}, bf16[256,1024]{1,0:T(8,128)(2,1)S(1)}, u32[]{:S(2)}, u32[]{:S(2)}) collective-permute-start(bf16[256,1024]{1,0:T(8,128)(2,1)S(1)} %get-tuple-element.43.own_ref), channel_id=1, source_target_pairs={{0,1},{1,2},{2,3},{3,4},{4,5},{5,6},{6,7},{7,8},{8,9},{9,10},{10,1... | collective-permute-start | bytes 1572872 | tf_op jit(solution)/shard_map/ppermute | solution.py:53
  53.3 27.4 %collective-permute-start.12 = (bf16[8,32,2048]{2,1,0:T(8,128)(2,1)S(1)}, bf16[8,32,2048]{2,1,0:T(8,128)(2,1)S(1)}, u32[]{:S(2)}, u32[]{:S(2)}) collective-permute-start(bf16[8,32,2048]{2,1,0:T(8,128)(2,1)S(1)} %get-tuple-element.48.refs_0_), channel_id=1, source_target_pairs={{0,8},{8,16},{16,24},{24,0},{1,9},{9,17},{17,25},{25,1},{2,10},{10... | collective-permute-start | bytes 3145736 | tf_op jit(solution)/shard_map/ppermute | solution.py:337
  59.3 21.4 %collective-permute-start.13 = (bf16[8,32,2048]{2,1,0:T(8,128)(2,1)S(1)}, bf16[8,32,2048]{2,1,0:T(8,128)(2,1)S(1)}, u32[]{:S(2)}, u32[]{:S(2)}) collective-permute-start(bf16[8,32,2048]{2,1,0:T(8,128)(2,1)S(1)} %get-tuple-element.48.refs_0_), channel_id=1, source_target_pairs={{0,24},{8,0},{16,8},{24,16},{1,25},{9,1},{17,9},{25,17},{2,26},{10... | collective-permute-start | bytes 3145736 | tf_op jit(solution)/shard_map/ppermute | solution.py:337
  59.3 22.0 %collective-permute-start.14 = (bf16[8,32,2048]{2,1,0:T(8,128)(2,1)S(1)}, bf16[8,32,2048]{2,1,0:T(8,128)(2,1)S(1)}, u32[]{:S(2)}, u32[]{:S(2)}) collective-permute-start(bf16[8,32,2048]{2,1,0:T(8,128)(2,1)S(1)} %get-tuple-element.48.refs_0_), channel_id=1, source_target_pairs={{0,32},{32,0},{1,33},{33,1},{2,34},{34,2},{3,35},{35,3},{4,36},{36... | collective-permute-start | bytes 3145736 | tf_op jit(solution)/shard_map/ppermute | solution.py:341
  59.7 21.5 %collective-permute-start.15 = (bf16[8,32,2048]{2,1,0:T(8,128)(2,1)S(1)}, bf16[8,32,2048]{2,1,0:T(8,128)(2,1)S(1)}, u32[]{:S(2)}, u32[]{:S(2)}) collective-permute-start(bf16[8,32,2048]{2,1,0:T(8,128)(2,1)S(1)} %get-tuple-element.49.refs_3_), channel_id=1, source_target_pairs={{0,160},{160,0},{32,128},{128,32},{1,161},{161,1},{33,129},{129,33... | collective-permute-start | bytes 3145736 | tf_op jit(solution)/shard_map/ppermute | solution.py:345
  62.2 9.2 %collective-permute-start.10 = (bf16[256,1024]{1,0:T(8,128)(2,1)S(1)}, bf16[256,1024]{1,0:T(8,128)(2,1)S(1)}, u32[]{:S(2)}, u32[]{:S(2)}) collective-permute-start(bf16[256,1024]{1,0:T(8,128)(2,1)S(1)} %get-tuple-element.43.own_ref), channel_id=1, source_target_pairs={{1,0},{2,1},{3,2},{4,3},{5,4},{6,5},{7,6},{8,7},{9,8},{10,9},{11,1... | collective-permute-start | bytes 1572872 | tf_op jit(solution)/shard_map/ppermute | solution.py:53
  75.8 12.2 %copy-start.11 = (s32[256]{0:T(256)S(1)}, s32[256]{0:T(256)}, u32[]{:S(2)}) copy-start(s32[256]{0:T(256)} %param.18) | copy-start | bytes 3076
  81.3 13.8 %collective-permute-start.16 = (bf16[4,32,2048]{2,1,0:T(8,128)(2,1)S(1)}, bf16[4,32,2048]{2,1,0:T(8,128)(2,1)S(1)}, u32[]{:S(2)}, u32[]{:S(2)}) collective-permute-start(bf16[4,32,2048]{2,1,0:T(8,128)(2,1)S(1)} %slice.10), channel_id=1, source_target_pairs={{0,32},{32,0},{1,33},{33,1},{2,34},{34,2},{3,35},{35,3},{4,36},{36... | collective-permute-start | bytes 1572872 | tf_op jit(solution)/shard_map/ppermute | solution.py:341
  82.5 12.7 %collective-permute-start.17 = (bf16[4,32,2048]{2,1,0:T(8,128)(2,1)S(1)}, bf16[4,32,2048]{2,1,0:T(8,128)(2,1)S(1)}, u32[]{:S(2)}, u32[]{:S(2)}) collective-permute-start(bf16[4,32,2048]{2,1,0:T(8,128)(2,1)S(1)} %slice.11), channel_id=1, source_target_pairs={{0,8},{8,16},{16,24},{24,0},{1,9},{9,17},{17,25},{25,1},{2,10},{10... | collective-permute-start | bytes 1572872 | tf_op jit(solution)/shard_map/ppermute | solution.py:337
  84.5 11.8 %collective-permute-start.18 = (bf16[4,32,2048]{2,1,0:T(8,128)(2,1)S(1)}, bf16[4,32,2048]{2,1,0:T(8,128)(2,1)S(1)}, u32[]{:S(2)}, u32[]{:S(2)}) collective-permute-start(bf16[4,32,2048]{2,1,0:T(8,128)(2,1)S(1)} %slice.12), channel_id=1, source_target_pairs={{0,160},{160,0},{32,128},{128,32},{1,161},{161,1},{33,129},{129,33... | collective-permute-start | bytes 1572872 | tf_op jit(solution)/shard_map/ppermute | solution.py:345
  86.6 11.0 %collective-permute-start.19 = (bf16[4,32,2048]{2,1,0:T(8,128)(2,1)S(1)}, bf16[4,32,2048]{2,1,0:T(8,128)(2,1)S(1)}, u32[]{:S(2)}, u32[]{:S(2)}) collective-permute-start(bf16[4,32,2048]{2,1,0:T(8,128)(2,1)S(1)} %slice.11), channel_id=1, source_target_pairs={{0,24},{8,0},{16,8},{24,16},{1,25},{9,1},{17,9},{25,17},{2,26},{10... | collective-permute-start | bytes 1572872 | tf_op jit(solution)/shard_map/ppermute | solution.py:337
  87.9 9.7 %copy-start.1 = (bf16[1024,1024]{1,0:T(8,128)(2,1)S(1)}, bf16[1024,1024]{1,0:T(8,128)(2,1)}, u32[]{:S(2)}) copy-start(bf16[1024,1024]{1,0:T(8,128)(2,1)} %out_ref.1) | copy-start | bytes 6291460
  98.6 8.3 %copy-start.12 = (bf16[1024,100]{0,1:T(8,128)(2,1)S(1)}, bf16[1024,100]{0,1:T(8,128)(2,1)}, u32[]{:S(2)}) copy-start(bf16[1024,100]{0,1:T(8,128)(2,1)} %param.27) | copy-start | bytes 614404
  98.6 2.0 %collective-permute-start.20 = (bf16[256,1024]{1,0:T(8,128)(2,1)S(1)}, bf16[256,1024]{1,0:T(8,128)(2,1)S(1)}, u32[]{:S(2)}, u32[]{:S(2)}) collective-permute-start(bf16[256,1024]{1,0:T(8,128)(2,1)S(1)} %get-tuple-element.59.own_ref), channel_id=1, source_target_pairs={{0,64},{64,0},{1,65},{65,1},{2,66},{66,2},{3,67},{67,3},{4,68},{68... | collective-permute-start | bytes 1572872 | tf_op jit(solution)/shard_map/ppermute | solution.py:57
  106.4 27.2 %copy-start.5 = (bf16[100,1024]{1,0:T(8,128)(2,1)S(1)}, bf16[100,1024]{1,0:T(8,128)(2,1)}, u32[]{:S(2)}) copy-start(bf16[100,1024]{1,0:T(8,128)(2,1)} %truth_ref.1) | copy-start | bytes 614404
  106.4 2.3 %collective-permute-start.21 = (bf16[256,1024]{1,0:T(8,128)(2,1)S(1)}, bf16[256,1024]{1,0:T(8,128)(2,1)S(1)}, u32[]{:S(2)}, u32[]{:S(2)}) collective-permute-start(bf16[256,1024]{1,0:T(8,128)(2,1)S(1)} %get-tuple-element.66), channel_id=1, source_target_pairs={{0,64},{64,0},{1,65},{65,1},{2,66},{66,2},{3,67},{67,3},{4,68},{68... | collective-permute-start | bytes 1572872 | tf_op jit(solution)/shard_map/ppermute | solution.py:57
  109.3 1.3 collective-permute-start.22
  110.6 6.8 %collective-permute-start.23 = (bf16[2,112,256]{2,1,0:T(8,128)(2,1)S(1)}, bf16[2,112,256]{2,1,0:T(8,128)(2,1)S(1)}, u32[]{:S(2)}, u32[]{:S(2)}) collective-permute-start(bf16[2,112,256]{2,1,0:T(8,128)(2,1)S(1)} %pad_maximum_fusion.3), channel_id=1, source_target_pairs={{0,128},{128,0},{1,129},{129,1},{2,130},{130,2},{3,131},{131,3},{4... | collective-permute-start | bytes 344072 | tf_op jit(solution)/shard_map/ppermute | solution.py:536
  117.4 16.1 %collective-permute-start.24 = (bf16[4,112,256]{2,1,0:T(8,128)(2,1)S(1)}, bf16[4,112,256]{2,1,0:T(8,128)(2,1)S(1)}, u32[]{:S(2)}, u32[]{:S(2)}) collective-permute-start(bf16[4,112,256]{2,1,0:T(8,128)(2,1)S(1)} %pad_maximum_fusion.1.refs_1_), channel_id=1, source_target_pairs={{0,1},{1,2},{2,3},{3,4},{4,5},{5,6},{6,7},{7,8},{8,9},{9,10},{10,1... | collective-permute-start | bytes 688136 | tf_op jit(solution)/shard_map/ppermute | solution.py:53
  117.5 16.0 %collective-permute-start.25 = (bf16[4,112,256]{2,1,0:T(8,128)(2,1)S(1)}, bf16[4,112,256]{2,1,0:T(8,128)(2,1)S(1)}, u32[]{:S(2)}, u32[]{:S(2)}) collective-permute-start(bf16[4,112,256]{2,1,0:T(8,128)(2,1)S(1)} %pad_maximum_fusion.1.refs_1_), channel_id=1, source_target_pairs={{1,0},{2,1},{3,2},{4,3},{5,4},{6,5},{7,6},{8,7},{9,8},{10,9},{11,1... | collective-permute-start | bytes 688136 | tf_op jit(solution)/shard_map/ppermute | solution.py:53

commit v2 on v1

--- a/solution.py
+++ b/solution.py
@@ -95,24 +95,37 @@
     )(place, slots, counts)
 
 
-def pooled_kernel(tally_ref, low_ref, own_ref, high_ref, count_ref, out_ref):
-    width = low_ref.shape[1]
+def pooled_kernel(
+    place_ref, tally_ref, own_ref, low_mine, low_other, high_mine, high_other, count_ref, out_ref
+):
+    width = own_ref.shape[1]
+    part = low_mine.shape[1]
+    mine = place_ref[6] * part
+    other = part - mine
     total = dot(own_ref[...], tally_ref[width : 2 * width, :])
-    total = total + dot(low_ref[...], tally_ref[:width, :])
-    total = total + dot(high_ref[...], tally_ref[2 * width :, :])
+    for first, held, side in (
+        (0, low_mine, mine),
+        (0, low_other, other),
+        (2 * width, high_mine, mine),
+        (2 * width, high_other, other),
+    ):
+        rows = pl.ds(pl.multiple_of(first + side, part), part)
+        total = total + dot(held[...], tally_ref[rows, :])
     out_ref[...] = (total / count_ref[...].astype(F32)).astype(BF16)
 
 
-def pool(tallies, low, own, high, counts):
+def pool(place, tallies, own, near, counts):
     nodes = tallies.shape[1]
     channels = own.shape[0]
+    vmem = pl.BlockSpec(memory_space=pltpu.VMEM)
     return pl.pallas_call(
         pooled_kernel,
         out_shape=jax.ShapeDtypeStruct((channels, nodes), BF16),
+        in_specs=[pl.BlockSpec(memory_space=pltpu.SMEM)] + [vmem] * 7,
         compiler_params=params(24),
         cost_estimate=SHORT,
         name="pooled",
-    )(tallies, low, own, high, counts)
+    )(place, tallies, own, *near, counts)
 
 
 def embed_kernel(pooled_ref, perturb_ref, embed_ref, gain_ref, start_ref, normed_ref):
@@ -468,7 +481,7 @@
             lax.axis_index(NODE[1]),
             lax.axis_index(NODE[2]),
             lax.axis_index(NODE[0]),
-            lax.axis_index(MEMBER),
+            core,
             (region - 1) * node_dev,
         ]
     ).astype(jnp.int32)
@@ -484,12 +497,15 @@
     tie = lax.optimization_barrier
 
     far_share = turn(share, NODE[1], 2)
-    state_low, state_high = neighbours(gridpoint_state)
+    part = grid_dev // 2
+    state_part = lax.dynamic_slice_in_dim(gridpoint_state, core * part, part, 1)
+    state_low, state_high = neighbours(state_part)
+    state_near = (state_low, other_core(state_low), state_high, other_core(state_high))
     tallies = encoder_tallies(place, encoder_slots.T, counts, 3 * grid_dev)
     tallies, far_share = tie((tallies, far_share))
     both = jnp.stack([share, far_share])
     ahead, behind = [turn(both, NODE[2], 1)], [turn(both, NODE[2], -1)]
-    pooled = pool(tallies, state_low, gridpoint_state, state_high, counts)
+    pooled = pool(place, tallies, gridpoint_state, state_near, counts)
     pooled, ahead[0], behind[0] = tie((pooled, ahead[0], behind[0]))
     start, normed = embed(pooled, perturb, embed_weight, norm_gains)
     for _ in range(2):

time: 136 us -> 132 us (0.971)
  waiting for transfers between devices: 52.6 us -> 49.6 us
  starting transfers between devices: 52.3 us -> 49.8 us
    ppermute x3, waiting for transfers between devices: 8.52 us -> 5.19 us  [neighbours(): lax.ppermute(block, NODE, forward)]
    ppermute x12, starting transfers between devices: 22.9 us -> 20.7 us  [turn(): lax.ppermute(block, axis, [(i, (i + step) % count) for i in range(count)])]
    ppermute x3 -> x5, waiting for transfers between devices: 4.75 us -> 6.05 us  [other_core(): return lax.ppermute(block, 'member_core', [(0, 1), (1, 0)])]
  transfers between devices with their start and end apart: 26 -> 28, of which waited for: 15 -> 17; matrix products, arithmetic and copies ran while one was open for 0% -> 1% of each run, Pallas kernels for 14% -> 14%
where the time goes in v2:
time: 132 us
  starting transfers between devices  49.8 us (38%)
  waiting for transfers between devices  49.6 us (38%)
  Pallas kernels  28.3 us (21%)
  local copies, waits for them, and re-layouts  3.56 us (3%)
    ppermute x12, waiting for transfers between devices, turn(): lax.ppermute(block, axis, [(i, (i + step) % count) for i in range(count)])  25.9 us
    ppermute x12, starting transfers between devices, turn(): lax.ppermute(block, axis, [(i, (i + step) % count) for i in range(count)])  20.7 us
    ppermute x3, starting transfers between devices, neighbours(): lax.ppermute(block, NODE, backward)  15.8 us
    pallas_call x1, Pallas kernels, attention(): pl.pallas_call(attention_kernel, out_shape=jax.ShapeDtypeStruct((nodes, w...  7.21 us
    ppermute x3, waiting for transfers between devices, neighbours(): lax.ppermute(block, NODE, backward)  6.12 us
    ppermute x5, waiting for transfers between devices, other_core(): return lax.ppermute(block, 'member_core', [(0, 1), (1, 0)])  6.05 us
    pallas_call x1, Pallas kernels, mlp_parts(): pl.pallas_call(mlp_kernel, out_shape=(jax.ShapeDtypeStruct((nodes, width)...  5.79 us
    ppermute x3, waiting for transfers between devices, neighbours(): lax.ppermute(block, NODE, forward)  5.19 us
  transfers between devices with their start and end apart: 28, of which 17 were waited for; matrix products, arithmetic and copies ran while one was open for 1% of the time, Pallas kernels for 14%

profile of v2, /device:TPU:8, one launch (start us, length us, event | category | flops | bytes accessed | tf_op | source)
XLA Modules:
  0.0 131.6 jit_solution(14657833063404773190)
XLA Ops:
  0.0 0.9 constant_dynamic-slice_fusion.1
  1.0 3.1 %collective-permute-start = (bf16[32,2048]{1,0:T(8,128)(2,1)S(1)}, bf16[32,2048]{1,0:T(8,128)(2,1)S(1)}, u32[]{:S(2)}, u32[]{:S(2)}) collective-permute-start(bf16[32,2048]{1,0:T(8,128)(2,1)S(1)} %get-tuple-element.68), channel_id=1, source_target_pairs={{0,16},{8,24},{16,0},{24,8},{1,17},{9,25},{17,1},{25,9},{2,18},{10... | collective-permute-start | bytes 393224 | tf_op jit(solution)/shard_map/ppermute | solution.py:350
  4.1 1.0 constant_dynamic-slice_fusion
  5.0 2.0 %collective-permute-start.1 = (bf16[218,512]{1,0:T(8,128)(2,1)S(1)}, bf16[218,512]{1,0:T(8,128)(2,1)S(1)}, u32[]{:S(2)}, u32[]{:S(2)}) collective-permute-start(bf16[218,512]{1,0:T(8,128)(2,1)S(1)} %constant_dynamic-slice_fusion), channel_id=1, source_target_pairs={{0,1},{1,2},{2,3},{3,4},{4,5},{5,6},{6,7},{7,8},{8,9},{9,10},{10,1... | collective-permute-start | bytes 669704 | tf_op jit(solution)/shard_map/ppermute | solution.py:53
  7.0 4.5 %collective-permute-start.3 = (bf16[218,512]{1,0:T(8,128)(2,1)S(1)}, bf16[218,512]{1,0:T(8,128)(2,1)S(1)}, u32[]{:S(2)}, u32[]{:S(2)}) collective-permute-start(bf16[218,512]{1,0:T(8,128)(2,1)S(1)} %constant_dynamic-slice_fusion), channel_id=1, source_target_pairs={{1,0},{2,1},{3,2},{4,3},{5,4},{6,5},{7,6},{8,7},{9,8},{10,9},{11,1... | collective-permute-start | bytes 669704 | tf_op jit(solution)/shard_map/ppermute | solution.py:53
  11.5 0.1 stack.49.place_ref.where_ref
  11.6 0.7 copy-done.7
  12.3 0.7 copy-done.9
  13.0 3.2 %encoder_tallies.1.tally_ref = bf16[3072,256]{1,0:T(8,128)(2,1)S(1)} custom-call(s32[8]{0:T(128)S(1)} %stack.49.place_ref.where_ref, s32[16,256]{1,0:T(8,128)S(1)} %bitcast.22, s32[1,256]{1,0:T(1,128)S(1)} %bitcast.24), custom_call_target="tpu_custom_call" | custom-call | flops 1 | bytes 1 | tf_op jit(solution)/shard_map/encoder_tallies/pallas_call | solution.py:88
  16.2 0.0 copy-start.3
  16.2 0.0 copy-start.4
  16.2 0.0 copy-start.6
  16.3 0.1 collective-permute-start.5
  16.4 3.2 %collective-permute-start.6 = (bf16[2,32,2048]{2,1,0:T(8,128)(2,1)S(1)}, bf16[2,32,2048]{2,1,0:T(8,128)(2,1)S(1)}, u32[]{:S(2)}, u32[]{:S(2)}) collective-permute-start(bf16[2,32,2048]{2,1,0:T(8,128)(2,1)S(1)} %pad_maximum_fusion.refs_0_), channel_id=1, source_target_pairs={{0,7},{1,0},{2,1},{3,2},{4,3},{5,4},{6,5},{7,6},{8,15},{9,8},{10,9... | collective-permute-start | bytes 786440 | tf_op jit(solution)/shard_map/ppermute | solution.py:350
  19.6 0.5 collective-permute-start.4
  20.1 1.0 collective-permute-done.2.low_other
  21.1 0.3 collective-permute-done.4.high_other
  21.4 1.1 pooled.1.pooled_ref
  22.5 2.5 %collective-permute-done.5.refs_7_ = bf16[2,32,2048]{2,1,0:T(8,128)(2,1)S(1)} collective-permute-done((bf16[2,32,2048]{2,1,0:T(8,128)(2,1)S(1)}, bf16[2,32,2048]{2,1,0:T(8,128)(2,1)S(1)}, u32[]{:S(2)}, u32[]{:S(2)}) %collective-permute-start.5) | collective-permute-done | bytes 262176 | tf_op jit(solution)/shard_map/ppermute | solution.py:350
  25.1 3.2 %collective-permute-start.9 = (bf16[2,32,2048]{2,1,0:T(8,128)(2,1)S(1)}, bf16[2,32,2048]{2,1,0:T(8,128)(2,1)S(1)}, u32[]{:S(2)}, u32[]{:S(2)}) collective-permute-start(bf16[2,32,2048]{2,1,0:T(8,128)(2,1)S(1)} %collective-permute-done.6.refs_1_), channel_id=1, source_target_pairs={{0,7},{1,0},{2,1},{3,2},{4,3},{5,4},{6,5},{7,6},{8,15},{9,8},{10,9... | collective-permute-start | bytes 786440 | tf_op jit(solution)/shard_map/ppermute | solution.py:350
  28.3 4.5 %collective-permute-done.7.refs_6_ = bf16[2,32,2048]{2,1,0:T(8,128)(2,1)S(1)} collective-permute-done((bf16[2,32,2048]{2,1,0:T(8,128)(2,1)S(1)}, bf16[2,32,2048]{2,1,0:T(8,128)(2,1)S(1)}, u32[]{:S(2)}, u32[]{:S(2)}) %collective-permute-start.7) | collective-permute-done | bytes 262176 | tf_op jit(solution)/shard_map/ppermute | solution.py:350
  32.8 3.2 %collective-permute-start.10 = (bf16[2,32,2048]{2,1,0:T(8,128)(2,1)S(1)}, bf16[2,32,2048]{2,1,0:T(8,128)(2,1)S(1)}, u32[]{:S(2)}, u32[]{:S(2)}) collective-permute-start(bf16[2,32,2048]{2,1,0:T(8,128)(2,1)S(1)} %collective-permute-done.9.refs_2_), channel_id=1, source_target_pairs={{0,7},{1,0},{2,1},{3,2},{4,3},{5,4},{6,5},{7,6},{8,15},{9,8},{10,9... | collective-permute-start | bytes 786440 | tf_op jit(solution)/shard_map/ppermute | solution.py:350
  36.1 0.6 embed.1
  36.7 3.7 %collective-permute-done.8.refs_5_ = bf16[2,32,2048]{2,1,0:T(8,128)(2,1)S(1)} collective-permute-done((bf16[2,32,2048]{2,1,0:T(8,128)(2,1)S(1)}, bf16[2,32,2048]{2,1,0:T(8,128)(2,1)S(1)}, u32[]{:S(2)}, u32[]{:S(2)}) %collective-permute-start.8) | collective-permute-done | bytes 262176 | tf_op jit(solution)/shard_map/ppermute | solution.py:350
  40.4 1.2 collective-permute-start.13
  41.6 2.0 %collective-permute-start.11 = (bf16[256,1024]{1,0:T(8,128)(2,1)S(1)}, bf16[256,1024]{1,0:T(8,128)(2,1)S(1)}, u32[]{:S(2)}, u32[]{:S(2)}) collective-permute-start(bf16[256,1024]{1,0:T(8,128)(2,1)S(1)} %get-tuple-element.43.own_ref), channel_id=1, source_target_pairs={{0,1},{1,2},{2,3},{3,4},{4,5},{5,6},{6,7},{7,8},{8,9},{9,10},{10,1... | collective-permute-start | bytes 1572872 | tf_op jit(solution)/shard_map/ppermute | solution.py:53
  43.7 7.2 %collective-permute-done.13.refs_4_ = bf16[2,32,2048]{2,1,0:T(8,128)(2,1)S(1)} collective-permute-done((bf16[2,32,2048]{2,1,0:T(8,128)(2,1)S(1)}, bf16[2,32,2048]{2,1,0:T(8,128)(2,1)S(1)}, u32[]{:S(2)}, u32[]{:S(2)}) %collective-permute-start.13) | collective-permute-done | bytes 262176 | tf_op jit(solution)/shard_map/ppermute | solution.py:350
  50.9 0.7 shards_in_order.1
  51.6 1.1 collective-permute-start.14
  52.7 2.2 %collective-permute-start.15 = (bf16[8,32,2048]{2,1,0:T(8,128)(2,1)S(1)}, bf16[8,32,2048]{2,1,0:T(8,128)(2,1)S(1)}, u32[]{:S(2)}, u32[]{:S(2)}) collective-permute-start(bf16[8,32,2048]{2,1,0:T(8,128)(2,1)S(1)} %get-tuple-element.48.refs_0_), channel_id=1, source_target_pairs={{0,24},{8,0},{16,8},{24,16},{1,25},{9,1},{17,9},{25,17},{2,26},{10... | collective-permute-start | bytes 3145736 | tf_op jit(solution)/shard_map/ppermute | solution.py:350
  54.9 1.6 %collective-permute-start.16 = (bf16[8,32,2048]{2,1,0:T(8,128)(2,1)S(1)}, bf16[8,32,2048]{2,1,0:T(8,128)(2,1)S(1)}, u32[]{:S(2)}, u32[]{:S(2)}) collective-permute-start(bf16[8,32,2048]{2,1,0:T(8,128)(2,1)S(1)} %get-tuple-element.48.refs_0_), channel_id=1, source_target_pairs={{0,32},{32,0},{1,33},{33,1},{2,34},{34,2},{3,35},{35,3},{4,36},{36... | collective-permute-start | bytes 3145736 | tf_op jit(solution)/shard_map/ppermute | solution.py:354
  56.5 1.6 %collective-permute-start.17 = (bf16[8,32,2048]{2,1,0:T(8,128)(2,1)S(1)}, bf16[8,32,2048]{2,1,0:T(8,128)(2,1)S(1)}, u32[]{:S(2)}, u32[]{:S(2)}) collective-permute-start(bf16[8,32,2048]{2,1,0:T(8,128)(2,1)S(1)} %get-tuple-element.49.refs_3_), channel_id=1, source_target_pairs={{0,160},{160,0},{32,128},{128,32},{1,161},{161,1},{33,129},{129,33... | collective-permute-start | bytes 3145736 | tf_op jit(solution)/shard_map/ppermute | solution.py:358
  58.0 0.2 collective-permute-done.11.low_ref
  58.2 2.6 %collective-permute-start.12 = (bf16[256,1024]{1,0:T(8,128)(2,1)S(1)}, bf16[256,1024]{1,0:T(8,128)(2,1)S(1)}, u32[]{:S(2)}, u32[]{:S(2)}) collective-permute-start(bf16[256,1024]{1,0:T(8,128)(2,1)S(1)} %get-tuple-element.43.own_ref), channel_id=1, source_target_pairs={{1,0},{2,1},{3,2},{4,3},{5,4},{6,5},{7,6},{8,7},{9,8},{10,9},{11,1... | collective-permute-start | bytes 1572872 | tf_op jit(solution)/shard_map/ppermute | solution.py:53
  60.8 1.8 %decoder_tallies.1.tally_ref = bf16[768,1024]{1,0:T(8,128)(2,1)S(1)} custom-call(s32[8]{0:T(128)S(1)} %stack.49.place_ref.where_ref, s32[4,1024]{1,0:T(4,128)S(1)} %bitcast.23), custom_call_target="tpu_custom_call" | custom-call | flops 1 | bytes 1 | tf_op jit(solution)/shard_map/decoder_tallies/pallas_call | solution.py:399
  62.6 6.1 %collective-permute-done.12.high_ref = bf16[256,1024]{1,0:T(8,128)(2,1)S(1)} collective-permute-done((bf16[256,1024]{1,0:T(8,128)(2,1)S(1)}, bf16[256,1024]{1,0:T(8,128)(2,1)S(1)}, u32[]{:S(2)}, u32[]{:S(2)}) %collective-permute-start.12) | collective-permute-done | bytes 524320 | tf_op jit(solution)/shard_map/ppermute | solution.py:53
  68.8 4.4 %qkv.1 = (bf16[256,1024]{1,0:T(8,128)(2,1)S(1)}, bf16[768,2048]{1,0:T(8,128)(2,1)S(1)}) custom-call(bf16[256,1024]{1,0:T(8,128)(2,1)S(1)} %collective-permute-done.11.low_ref, bf16[256,1024]{1,0:T(8,128)(2,1)S(1)} %get-tuple-element.43.own_ref, bf16[256,1024]{1,0:T(8,128)(2,1)S(1)} %collective-permute-done.12.high_ref, bf16[1024,3072]{1,0:T(8,128)(2,1)S(1)} %copy-done), custom_call_target="tpu_custom_call" | custom-call | flops 1 | bytes 1 | tf_op jit(solution)/shard_map/qkv/pallas_call | solution.py:171
  73.2 0.0 copy-start.11
  73.2 5.7 %collective-permute-done.14.refs_1_ = bf16[8,32,2048]{2,1,0:T(8,128)(2,1)S(1)} collective-permute-done((bf16[8,32,2048]{2,1,0:T(8,128)(2,1)S(1)}, bf16[8,32,2048]{2,1,0:T(8,128)(2,1)S(1)}, u32[]{:S(2)}, u32[]{:S(2)}) %collective-permute-start.14) | collective-permute-done | bytes 1048608 | tf_op jit(solution)/shard_map/ppermute | solution.py:350
  78.9 1.2 collective-permute-done.16.refs_4_
  80.1 1.1 collective-permute-start.18
  81.3 0.1 collective-permute-start.19
  81.4 1.9 %collective-permute-start.20 = (bf16[4,32,2048]{2,1,0:T(8,128)(2,1)S(1)}, bf16[4,32,2048]{2,1,0:T(8,128)(2,1)S(1)}, u32[]{:S(2)}, u32[]{:S(2)}) collective-permute-start(bf16[4,32,2048]{2,1,0:T(8,128)(2,1)S(1)} %slice.12), channel_id=1, source_target_pairs={{0,160},{160,0},{32,128},{128,32},{1,161},{161,1},{33,129},{129,33... | collective-permute-start | bytes 1572872 | tf_op jit(solution)/shard_map/ppermute | solution.py:358
  83.3 3.2 %collective-permute-start.21 = (bf16[4,32,2048]{2,1,0:T(8,128)(2,1)S(1)}, bf16[4,32,2048]{2,1,0:T(8,128)(2,1)S(1)}, u32[]{:S(2)}, u32[]{:S(2)}) collective-permute-start(bf16[4,32,2048]{2,1,0:T(8,128)(2,1)S(1)} %slice.11), channel_id=1, source_target_pairs={{0,24},{8,0},{16,8},{24,16},{1,25},{9,1},{17,9},{25,17},{2,26},{10... | collective-permute-start | bytes 1572872 | tf_op jit(solution)/shard_map/ppermute | solution.py:350
  86.5 7.2 %attention.1.attended_ref = bf16[256,1024]{1,0:T(8,128)(2,1)S(1)} custom-call(s32[8]{0:T(128)S(1)} %stack.49.place_ref.where_ref, bf16[256,1024]{1,0:T(8,128)(2,1)S(1)} %get-tuple-element.52.query_ref, bf16[768,2048]{1,0:T(8,128)(2,1)S(1)} %get-tuple-element.53.kv_ref, s32[1,256]{1,0:T(1,128)S(1)} %bitcast.26), custom_call_target="tpu_custom_call" | custom-call | flops 1 | bytes 1 | tf_op jit(solution)/shard_map/attention/pallas_call | solution.py:254
  93.8 1.0 collective-permute-done.19.refs_6_
  94.8 1.1 collective-permute-done.21.refs_8_
  95.9 1.0 middle.1
  96.9 0.0 copy-start.12
  96.9 0.1 collective-permute-start.22
  97.0 1.9 %collective-permute-done.22.other_ref = bf16[256,1024]{1,0:T(8,128)(2,1)S(1)} collective-permute-done((bf16[256,1024]{1,0:T(8,128)(2,1)S(1)}, bf16[256,1024]{1,0:T(8,128)(2,1)S(1)}, u32[]{:S(2)}, u32[]{:S(2)}) %collective-permute-start.22) | collective-permute-done | bytes 524320 | tf_op jit(solution)/shard_map/ppermute | solution.py:57
  98.9 5.8 %mlp_parts.1 = (f32[256,1024]{1,0:T(8,128)S(1)}, bf16[256,1024]{1,0:T(8,128)(2,1)S(1)}) custom-call(s32[8]{0:T(128)S(1)} %stack.49.place_ref.where_ref, bf16[256,1024]{1,0:T(8,128)(2,1)S(1)} %get-tuple-element.59.own_ref, bf16[256,1024]{1,0:T(8,128)(2,1)S(1)} %collective-permute-done.22.other_ref, bf16[8,32,2048]{2,1,0:T(8,128)(2,1)S(1)} %get-tuple-element.48.refs_0_, ...), custom_call_target="tpu_custom_call" | custom-call | flops 1 | bytes 1 | tf_op jit(solution)/shard_map/mlp_parts/pallas_call | solution.py:331
  104.7 0.0 copy-start.5
  104.7 0.5 collective-permute-start.23
  105.2 1.8 %collective-permute-done.23.other_ref = bf16[256,1024]{1,0:T(8,128)(2,1)S(1)} collective-permute-done((bf16[256,1024]{1,0:T(8,128)(2,1)S(1)}, bf16[256,1024]{1,0:T(8,128)(2,1)S(1)}, u32[]{:S(2)}, u32[]{:S(2)}) %collective-permute-start.23) | collective-permute-done | bytes 524320 | tf_op jit(solution)/shard_map/ppermute | solution.py:57
  107.0 0.6 final_head.1
  107.6 0.2 collective-permute-start.24
  107.8 1.1 collective-permute-done.24
  108.9 1.7 %collective-permute-start.25 = (bf16[2,112,256]{2,1,0:T(8,128)(2,1)S(1)}, bf16[2,112,256]{2,1,0:T(8,128)(2,1)S(1)}, u32[]{:S(2)}, u32[]{:S(2)}) collective-permute-start(bf16[2,112,256]{2,1,0:T(8,128)(2,1)S(1)} %pad_maximum_fusion.3), channel_id=1, source_target_pairs={{0,128},{128,0},{1,129},{129,1},{2,130},{130,2},{3,131},{131,3},{4... | collective-permute-start | bytes 344072 | tf_op jit(solution)/shard_map/ppermute | solution.py:552
  110.6 5.1 %collective-permute-done.25 = bf16[2,112,256]{2,1,0:T(8,128)(2,1)S(1)} collective-permute-done((bf16[2,112,256]{2,1,0:T(8,128)(2,1)S(1)}, bf16[2,112,256]{2,1,0:T(8,128)(2,1)S(1)}, u32[]{:S(2)}, u32[]{:S(2)}) %collective-permute-start.25) | collective-permute-done | bytes 114720 | tf_op jit(solution)/shard_map/ppermute | solution.py:552
  115.8 0.1 collective-permute-start.26
  115.9 8.7 %collective-permute-start.27 = (bf16[4,112,256]{2,1,0:T(8,128)(2,1)S(1)}, bf16[4,112,256]{2,1,0:T(8,128)(2,1)S(1)}, u32[]{:S(2)}, u32[]{:S(2)}) collective-permute-start(bf16[4,112,256]{2,1,0:T(8,128)(2,1)S(1)} %pad_maximum_fusion.1.refs_1_), channel_id=1, source_target_pairs={{1,0},{2,1},{3,2},{4,3},{5,4},{6,5},{7,6},{8,7},{9,8},{10,9},{11,1... | collective-permute-start | bytes 688136 | tf_op jit(solution)/shard_map/ppermute | solution.py:53
  124.6 5.0 %collective-permute-done.26.refs_0_ = bf16[4,112,256]{2,1,0:T(8,128)(2,1)S(1)} collective-permute-done((bf16[4,112,256]{2,1,0:T(8,128)(2,1)S(1)}, bf16[4,112,256]{2,1,0:T(8,128)(2,1)S(1)}, u32[]{:S(2)}, u32[]{:S(2)}) %collective-permute-start.26) | collective-permute-done | bytes 229408 | tf_op jit(solution)/shard_map/ppermute | solution.py:53
  129.6 2.0 %decoder_crps.1 = f32[100,1,1024]{2,1,0:T(1,128)} custom-call(bf16[768,1024]{1,0:T(8,128)(2,1)S(1)} %decoder_tallies.1.tally_ref, bf16[218,1024]{1,0:T(8,128)(2,1)S(1)} %copy-done.1, bf16[100,1024]{1,0:T(8,128)(2,1)S(1)} %copy-done.5, bf16[4,112,256]{2,1,0:T(8,128)(2,1)S(1)} %collective-permute-done.26.refs_0_, ...), custom_call_target="tpu_custom_call" | custom-call | flops 1 | bytes 1 | tf_op jit(solution)/shard_map/decoder_crps/pallas_call | solution.py:442
  (40 shorter events, 0.3 us)
Async XLA Ops:
  0.0 21.4 %copy-start.1 = (bf16[218,1024]{1,0:T(8,128)(2,1)S(1)}, bf16[218,1024]{1,0:T(8,128)(2,1)}, u32[]{:S(2)}) copy-start(bf16[218,1024]{1,0:T(8,128)(2,1)} %state_ref.1) | copy-start | bytes 1339396
  0.0 21.4 %copy-start.10 = (s32[256]{0:T(256)S(1)}, s32[256]{0:T(256)}, u32[]{:S(2)}) copy-start(s32[256]{0:T(256)} %param.17) | copy-start | bytes 3076
  1.0 15.3 %collective-permute-start = (bf16[32,2048]{1,0:T(8,128)(2,1)S(1)}, bf16[32,2048]{1,0:T(8,128)(2,1)S(1)}, u32[]{:S(2)}, u32[]{:S(2)}) collective-permute-start(bf16[32,2048]{1,0:T(8,128)(2,1)S(1)} %get-tuple-element.68), channel_id=1, source_target_pairs={{0,16},{8,24},{16,0},{24,8},{1,17},{9,25},{17,1},{25,9},{2,18},{10... | collective-permute-start | bytes 393224 | tf_op jit(solution)/shard_map/ppermute | solution.py:350
  5.0 14.6 %collective-permute-start.1 = (bf16[218,512]{1,0:T(8,128)(2,1)S(1)}, bf16[218,512]{1,0:T(8,128)(2,1)S(1)}, u32[]{:S(2)}, u32[]{:S(2)}) collective-permute-start(bf16[218,512]{1,0:T(8,128)(2,1)S(1)} %constant_dynamic-slice_fusion), channel_id=1, source_target_pairs={{0,1},{1,2},{2,3},{3,4},{4,5},{5,6},{6,7},{7,8},{8,9},{9,10},{10,1... | collective-permute-start | bytes 669704 | tf_op jit(solution)/shard_map/ppermute | solution.py:53
  7.0 12.6 %collective-permute-start.3 = (bf16[218,512]{1,0:T(8,128)(2,1)S(1)}, bf16[218,512]{1,0:T(8,128)(2,1)S(1)}, u32[]{:S(2)}, u32[]{:S(2)}) collective-permute-start(bf16[218,512]{1,0:T(8,128)(2,1)S(1)} %constant_dynamic-slice_fusion), channel_id=1, source_target_pairs={{1,0},{2,1},{3,2},{4,3},{5,4},{6,5},{7,6},{8,7},{9,8},{10,9},{11,1... | collective-permute-start | bytes 669704 | tf_op jit(solution)/shard_map/ppermute | solution.py:53
  11.6 0.7 copy-start.7
  12.3 0.7 copy-start.9
  16.2 19.9 %copy-start.3 = (bf16[1,256,1024]{2,1,0:T(8,128)(2,1)S(1)}, bf16[1,256,1024]{2,1,0:T(8,128)(2,1)}, u32[]{:S(2)}) copy-start(bf16[1,256,1024]{2,1,0:T(8,128)(2,1)} %param.20) | copy-start | bytes 1572868
  16.2 19.9 %copy-start.4 = (bf16[218,1024]{1,0:T(8,128)(2,1)S(1)}, bf16[218,1024]{1,0:T(8,128)(2,1)}, u32[]{:S(2)}) copy-start(bf16[218,1024]{1,0:T(8,128)(2,1)} %embed_ref.1) | copy-start | bytes 1339396
  16.2 19.9 %copy-start.6 = (f32[3,1024]{1,0:T(4,128)S(1)}, f32[3,1024]{1,0:T(4,128)}, u32[]{:S(2)}) copy-start(f32[3,1024]{1,0:T(4,128)} %gain_ref.5) | copy-start | bytes 36868
  16.3 8.8 %collective-permute-start.5 = (bf16[2,32,2048]{2,1,0:T(8,128)(2,1)S(1)}, bf16[2,32,2048]{2,1,0:T(8,128)(2,1)S(1)}, u32[]{:S(2)}, u32[]{:S(2)}) collective-permute-start(bf16[2,32,2048]{2,1,0:T(8,128)(2,1)S(1)} %pad_maximum_fusion.refs_0_), channel_id=1, source_target_pairs={{0,1},{1,2},{2,3},{3,4},{4,5},{5,6},{6,7},{7,0},{8,9},{9,10},{10,1... | collective-permute-start | bytes 786440 | tf_op jit(solution)/shard_map/ppermute | solution.py:350
  16.4 8.7 %collective-permute-start.6 = (bf16[2,32,2048]{2,1,0:T(8,128)(2,1)S(1)}, bf16[2,32,2048]{2,1,0:T(8,128)(2,1)S(1)}, u32[]{:S(2)}, u32[]{:S(2)}) collective-permute-start(bf16[2,32,2048]{2,1,0:T(8,128)(2,1)S(1)} %pad_maximum_fusion.refs_0_), channel_id=1, source_target_pairs={{0,7},{1,0},{2,1},{3,2},{4,3},{5,4},{6,5},{7,6},{8,15},{9,8},{10,9... | collective-permute-start | bytes 786440 | tf_op jit(solution)/shard_map/ppermute | solution.py:350
  19.6 1.5 %collective-permute-start.2 = (bf16[218,512]{1,0:T(8,128)(2,1)S(1)}, bf16[218,512]{1,0:T(8,128)(2,1)S(1)}, u32[]{:S(2)}, u32[]{:S(2)}) collective-permute-start(bf16[218,512]{1,0:T(8,128)(2,1)S(1)} %collective-permute-done.1.low_mine), channel_id=1, source_target_pairs={{0,64},{64,0},{1,65},{65,1},{2,66},{66,2},{3,67},{67,3},{4,68},{68... | collective-permute-start | bytes 669704 | tf_op jit(solution)/shard_map/ppermute | solution.py:57
  19.6 1.8 %collective-permute-start.4 = (bf16[218,512]{1,0:T(8,128)(2,1)S(1)}, bf16[218,512]{1,0:T(8,128)(2,1)S(1)}, u32[]{:S(2)}, u32[]{:S(2)}) collective-permute-start(bf16[218,512]{1,0:T(8,128)(2,1)S(1)} %collective-permute-done.3.high_mine), channel_id=1, source_target_pairs={{0,64},{64,0},{1,65},{65,1},{2,66},{66,2},{3,67},{67,3},{4,68},{68... | collective-permute-start | bytes 669704 | tf_op jit(solution)/shard_map/ppermute | solution.py:57
  21.1 39.7 %copy-start.8 = (s32[1024,4]{0,1:T(4,128)S(1)}, s32[1024,4]{0,1:T(4,128)}, u32[]{:S(2)}) copy-start(s32[1024,4]{0,1:T(4,128)} %param.19) | copy-start | bytes 49156
  21.4 47.3 %copy-start = (bf16[1024,3072]{1,0:T(8,128)(2,1)S(1)}, bf16[1024,3072]{1,0:T(8,128)(2,1)}, u32[]{:S(2)}) copy-start(bf16[1024,3072]{1,0:T(8,128)(2,1)} %qkv_hbm.1) | copy-start | bytes 18874372
  25.1 7.8 %collective-permute-start.7 = (bf16[2,32,2048]{2,1,0:T(8,128)(2,1)S(1)}, bf16[2,32,2048]{2,1,0:T(8,128)(2,1)S(1)}, u32[]{:S(2)}, u32[]{:S(2)}) collective-permute-start(bf16[2,32,2048]{2,1,0:T(8,128)(2,1)S(1)} %collective-permute-done.5.refs_7_), channel_id=1, source_target_pairs={{0,1},{1,2},{2,3},{3,4},{4,5},{5,6},{6,7},{7,0},{8,9},{9,10},{10,1... | collective-permute-start | bytes 786440 | tf_op jit(solution)/shard_map/ppermute | solution.py:350
  25.1 7.8 %collective-permute-start.9 = (bf16[2,32,2048]{2,1,0:T(8,128)(2,1)S(1)}, bf16[2,32,2048]{2,1,0:T(8,128)(2,1)S(1)}, u32[]{:S(2)}, u32[]{:S(2)}) collective-permute-start(bf16[2,32,2048]{2,1,0:T(8,128)(2,1)S(1)} %collective-permute-done.6.refs_1_), channel_id=1, source_target_pairs={{0,7},{1,0},{2,1},{3,2},{4,3},{5,4},{6,5},{7,6},{8,15},{9,8},{10,9... | collective-permute-start | bytes 786440 | tf_op jit(solution)/shard_map/ppermute | solution.py:350
  32.8 7.6 %collective-permute-start.8 = (bf16[2,32,2048]{2,1,0:T(8,128)(2,1)S(1)}, bf16[2,32,2048]{2,1,0:T(8,128)(2,1)S(1)}, u32[]{:S(2)}, u32[]{:S(2)}) collective-permute-start(bf16[2,32,2048]{2,1,0:T(8,128)(2,1)S(1)} %collective-permute-done.7.refs_6_), channel_id=1, source_target_pairs={{0,1},{1,2},{2,3},{3,4},{4,5},{5,6},{6,7},{7,0},{8,9},{9,10},{10,1... | collective-permute-start | bytes 786440 | tf_op jit(solution)/shard_map/ppermute | solution.py:350
  32.8 7.6 %collective-permute-start.10 = (bf16[2,32,2048]{2,1,0:T(8,128)(2,1)S(1)}, bf16[2,32,2048]{2,1,0:T(8,128)(2,1)S(1)}, u32[]{:S(2)}, u32[]{:S(2)}) collective-permute-start(bf16[2,32,2048]{2,1,0:T(8,128)(2,1)S(1)} %collective-permute-done.9.refs_2_), channel_id=1, source_target_pairs={{0,7},{1,0},{2,1},{3,2},{4,3},{5,4},{6,5},{7,6},{8,15},{9,8},{10,9... | collective-permute-start | bytes 786440 | tf_op jit(solution)/shard_map/ppermute | solution.py:350
  40.4 10.5 %collective-permute-start.13 = (bf16[2,32,2048]{2,1,0:T(8,128)(2,1)S(1)}, bf16[2,32,2048]{2,1,0:T(8,128)(2,1)S(1)}, u32[]{:S(2)}, u32[]{:S(2)}) collective-permute-start(bf16[2,32,2048]{2,1,0:T(8,128)(2,1)S(1)} %collective-permute-done.8.refs_5_), channel_id=1, source_target_pairs={{0,1},{1,2},{2,3},{3,4},{4,5},{5,6},{6,7},{7,0},{8,9},{9,10},{10,1... | collective-permute-start | bytes 786440 | tf_op jit(solution)/shard_map/ppermute | solution.py:350
  41.6 16.6 %collective-permute-start.11 = (bf16[256,1024]{1,0:T(8,128)(2,1)S(1)}, bf16[256,1024]{1,0:T(8,128)(2,1)S(1)}, u32[]{:S(2)}, u32[]{:S(2)}) collective-permute-start(bf16[256,1024]{1,0:T(8,128)(2,1)S(1)} %get-tuple-element.43.own_ref), channel_id=1, source_target_pairs={{0,1},{1,2},{2,3},{3,4},{4,5},{5,6},{6,7},{7,8},{8,9},{9,10},{10,1... | collective-permute-start | bytes 1572872 | tf_op jit(solution)/shard_map/ppermute | solution.py:53
  51.6 27.3 %collective-permute-start.14 = (bf16[8,32,2048]{2,1,0:T(8,128)(2,1)S(1)}, bf16[8,32,2048]{2,1,0:T(8,128)(2,1)S(1)}, u32[]{:S(2)}, u32[]{:S(2)}) collective-permute-start(bf16[8,32,2048]{2,1,0:T(8,128)(2,1)S(1)} %get-tuple-element.48.refs_0_), channel_id=1, source_target_pairs={{0,8},{8,16},{16,24},{24,0},{1,9},{9,17},{17,25},{25,1},{2,10},{10... | collective-permute-start | bytes 3145736 | tf_op jit(solution)/shard_map/ppermute | solution.py:350
  52.7 26.2 %collective-permute-start.15 = (bf16[8,32,2048]{2,1,0:T(8,128)(2,1)S(1)}, bf16[8,32,2048]{2,1,0:T(8,128)(2,1)S(1)}, u32[]{:S(2)}, u32[]{:S(2)}) collective-permute-start(bf16[8,32,2048]{2,1,0:T(8,128)(2,1)S(1)} %get-tuple-element.48.refs_0_), channel_id=1, source_target_pairs={{0,24},{8,0},{16,8},{24,16},{1,25},{9,1},{17,9},{25,17},{2,26},{10... | collective-permute-start | bytes 3145736 | tf_op jit(solution)/shard_map/ppermute | solution.py:350
  54.9 25.2 %collective-permute-start.16 = (bf16[8,32,2048]{2,1,0:T(8,128)(2,1)S(1)}, bf16[8,32,2048]{2,1,0:T(8,128)(2,1)S(1)}, u32[]{:S(2)}, u32[]{:S(2)}) collective-permute-start(bf16[8,32,2048]{2,1,0:T(8,128)(2,1)S(1)} %get-tuple-element.48.refs_0_), channel_id=1, source_target_pairs={{0,32},{32,0},{1,33},{33,1},{2,34},{34,2},{3,35},{35,3},{4,36},{36... | collective-permute-start | bytes 3145736 | tf_op jit(solution)/shard_map/ppermute | solution.py:354
  56.5 23.6 %collective-permute-start.17 = (bf16[8,32,2048]{2,1,0:T(8,128)(2,1)S(1)}, bf16[8,32,2048]{2,1,0:T(8,128)(2,1)S(1)}, u32[]{:S(2)}, u32[]{:S(2)}) collective-permute-start(bf16[8,32,2048]{2,1,0:T(8,128)(2,1)S(1)} %get-tuple-element.49.refs_3_), channel_id=1, source_target_pairs={{0,160},{160,0},{32,128},{128,32},{1,161},{161,1},{33,129},{129,33... | collective-permute-start | bytes 3145736 | tf_op jit(solution)/shard_map/ppermute | solution.py:358
  58.2 10.5 %collective-permute-start.12 = (bf16[256,1024]{1,0:T(8,128)(2,1)S(1)}, bf16[256,1024]{1,0:T(8,128)(2,1)S(1)}, u32[]{:S(2)}, u32[]{:S(2)}) collective-permute-start(bf16[256,1024]{1,0:T(8,128)(2,1)S(1)} %get-tuple-element.43.own_ref), channel_id=1, source_target_pairs={{1,0},{2,1},{3,2},{4,3},{5,4},{6,5},{7,6},{8,7},{9,8},{10,9},{11,1... | collective-permute-start | bytes 1572872 | tf_op jit(solution)/shard_map/ppermute | solution.py:53
  73.2 13.4 %copy-start.11 = (s32[256]{0:T(256)S(1)}, s32[256]{0:T(256)}, u32[]{:S(2)}) copy-start(s32[256]{0:T(256)} %param.18) | copy-start | bytes 3076
  80.1 13.6 %collective-permute-start.18 = (bf16[4,32,2048]{2,1,0:T(8,128)(2,1)S(1)}, bf16[4,32,2048]{2,1,0:T(8,128)(2,1)S(1)}, u32[]{:S(2)}, u32[]{:S(2)}) collective-permute-start(bf16[4,32,2048]{2,1,0:T(8,128)(2,1)S(1)} %slice.10), channel_id=1, source_target_pairs={{0,32},{32,0},{1,33},{33,1},{2,34},{34,2},{3,35},{35,3},{4,36},{36... | collective-permute-start | bytes 1572872 | tf_op jit(solution)/shard_map/ppermute | solution.py:354
  81.3 13.5 %collective-permute-start.19 = (bf16[4,32,2048]{2,1,0:T(8,128)(2,1)S(1)}, bf16[4,32,2048]{2,1,0:T(8,128)(2,1)S(1)}, u32[]{:S(2)}, u32[]{:S(2)}) collective-permute-start(bf16[4,32,2048]{2,1,0:T(8,128)(2,1)S(1)} %slice.11), channel_id=1, source_target_pairs={{0,8},{8,16},{16,24},{24,0},{1,9},{9,17},{17,25},{25,1},{2,10},{10... | collective-permute-start | bytes 1572872 | tf_op jit(solution)/shard_map/ppermute | solution.py:350
  81.4 13.3 %collective-permute-start.20 = (bf16[4,32,2048]{2,1,0:T(8,128)(2,1)S(1)}, bf16[4,32,2048]{2,1,0:T(8,128)(2,1)S(1)}, u32[]{:S(2)}, u32[]{:S(2)}) collective-permute-start(bf16[4,32,2048]{2,1,0:T(8,128)(2,1)S(1)} %slice.12), channel_id=1, source_target_pairs={{0,160},{160,0},{32,128},{128,32},{1,161},{161,1},{33,129},{129,33... | collective-permute-start | bytes 1572872 | tf_op jit(solution)/shard_map/ppermute | solution.py:358
  83.3 12.6 %collective-permute-start.21 = (bf16[4,32,2048]{2,1,0:T(8,128)(2,1)S(1)}, bf16[4,32,2048]{2,1,0:T(8,128)(2,1)S(1)}, u32[]{:S(2)}, u32[]{:S(2)}) collective-permute-start(bf16[4,32,2048]{2,1,0:T(8,128)(2,1)S(1)} %slice.11), channel_id=1, source_target_pairs={{0,24},{8,0},{16,8},{24,16},{1,25},{9,1},{17,9},{25,17},{2,26},{10... | collective-permute-start | bytes 1572872 | tf_op jit(solution)/shard_map/ppermute | solution.py:350
  86.5 9.4 %copy-start.2 = (bf16[1024,1024]{1,0:T(8,128)(2,1)S(1)}, bf16[1024,1024]{1,0:T(8,128)(2,1)}, u32[]{:S(2)}) copy-start(bf16[1024,1024]{1,0:T(8,128)(2,1)} %out_ref.1) | copy-start | bytes 6291460
  96.9 8.3 %copy-start.12 = (bf16[1024,100]{0,1:T(8,128)(2,1)S(1)}, bf16[1024,100]{0,1:T(8,128)(2,1)}, u32[]{:S(2)}) copy-start(bf16[1024,100]{0,1:T(8,128)(2,1)} %param.27) | copy-start | bytes 614404
  96.9 2.0 %collective-permute-start.22 = (bf16[256,1024]{1,0:T(8,128)(2,1)S(1)}, bf16[256,1024]{1,0:T(8,128)(2,1)S(1)}, u32[]{:S(2)}, u32[]{:S(2)}) collective-permute-start(bf16[256,1024]{1,0:T(8,128)(2,1)S(1)} %get-tuple-element.59.own_ref), channel_id=1, source_target_pairs={{0,64},{64,0},{1,65},{65,1},{2,66},{66,2},{3,67},{67,3},{4,68},{68... | collective-permute-start | bytes 1572872 | tf_op jit(solution)/shard_map/ppermute | solution.py:57
  104.7 24.9 %copy-start.5 = (bf16[100,1024]{1,0:T(8,128)(2,1)S(1)}, bf16[100,1024]{1,0:T(8,128)(2,1)}, u32[]{:S(2)}) copy-start(bf16[100,1024]{1,0:T(8,128)(2,1)} %truth_ref.1) | copy-start | bytes 614404
  104.7 2.3 %collective-permute-start.23 = (bf16[256,1024]{1,0:T(8,128)(2,1)S(1)}, bf16[256,1024]{1,0:T(8,128)(2,1)S(1)}, u32[]{:S(2)}, u32[]{:S(2)}) collective-permute-start(bf16[256,1024]{1,0:T(8,128)(2,1)S(1)} %get-tuple-element.66), channel_id=1, source_target_pairs={{0,64},{64,0},{1,65},{65,1},{2,66},{66,2},{3,67},{67,3},{4,68},{68... | collective-permute-start | bytes 1572872 | tf_op jit(solution)/shard_map/ppermute | solution.py:57
  107.6 1.3 %collective-permute-start.24 = (bf16[112,256]{1,0:T(8,128)(2,1)S(1)}, bf16[112,256]{1,0:T(8,128)(2,1)S(1)}, u32[]{:S(2)}, u32[]{:S(2)}) collective-permute-start(bf16[112,256]{1,0:T(8,128)(2,1)S(1)} %final_head.1), channel_id=1, source_target_pairs={{0,64},{64,0},{1,65},{65,1},{2,66},{66,2},{3,67},{67,3},{4,68},{68... | collective-permute-start | bytes 172040 | tf_op jit(solution)/shard_map/ppermute | solution.py:57
  108.9 6.8 %collective-permute-start.25 = (bf16[2,112,256]{2,1,0:T(8,128)(2,1)S(1)}, bf16[2,112,256]{2,1,0:T(8,128)(2,1)S(1)}, u32[]{:S(2)}, u32[]{:S(2)}) collective-permute-start(bf16[2,112,256]{2,1,0:T(8,128)(2,1)S(1)} %pad_maximum_fusion.3), channel_id=1, source_target_pairs={{0,128},{128,0},{1,129},{129,1},{2,130},{130,2},{3,131},{131,3},{4... | collective-permute-start | bytes 344072 | tf_op jit(solution)/shard_map/ppermute | solution.py:552
  115.8 13.8 %collective-permute-start.26 = (bf16[4,112,256]{2,1,0:T(8,128)(2,1)S(1)}, bf16[4,112,256]{2,1,0:T(8,128)(2,1)S(1)}, u32[]{:S(2)}, u32[]{:S(2)}) collective-permute-start(bf16[4,112,256]{2,1,0:T(8,128)(2,1)S(1)} %pad_maximum_fusion.1.refs_1_), channel_id=1, source_target_pairs={{0,1},{1,2},{2,3},{3,4},{4,5},{5,6},{6,7},{7,8},{8,9},{9,10},{10,1... | collective-permute-start | bytes 688136 | tf_op jit(solution)/shard_map/ppermute | solution.py:53
  115.9 13.7 %collective-permute-start.27 = (bf16[4,112,256]{2,1,0:T(8,128)(2,1)S(1)}, bf16[4,112,256]{2,1,0:T(8,128)(2,1)S(1)}, u32[]{:S(2)}, u32[]{:S(2)}) collective-permute-start(bf16[4,112,256]{2,1,0:T(8,128)(2,1)S(1)} %pad_maximum_fusion.1.refs_1_), channel_id=1, source_target_pairs={{1,0},{2,1},{3,2},{4,3},{5,4},{6,5},{7,6},{8,7},{9,8},{10,9},{11,1... | collective-permute-start | bytes 688136 | tf_op jit(solution)/shard_map/ppermute | solution.py:53
